TPU v7x, 128 devices: a whole 4x4x4 slice. The times are simulated.
128 devices in a mesh: lat: 8 (over z, core), lon: 16 (over y, x).
Axes of the slice: x: 4, y: 4, z: 4, core: 2. Of those that a mesh axis runs over, the one named last changes fastest.
Arguments:
- tokens: bfloat16 [128, 1024, 512], P('lat', 'lon'), may hold values from -6 to 6
- norm_gain: float32 [512], replicated, may hold values from 0.25 to 1.75
- w_query: bfloat16 [512, 512], replicated, may hold values from -1 to 1
- w_key: bfloat16 [512, 512], replicated, may hold values from -1 to 1
- w_value: bfloat16 [512, 512], replicated, may hold values from -0.25 to 0.25
- w_out: bfloat16 [512, 512], replicated, may hold values from -0.25 to 0.25
- pool_weight: bfloat16 [4, 64], replicated, may hold values from -0.75 to 0.75
- head_scale: float32 [8], replicated, may hold values from 0.5 to 32
- far_ids: int32 [16, 128, 48], P('lat', 'lon'), may hold values from 0 to 2047, as said below
- far_mask: int32 [16, 128, 48], P('lat', 'lon'), may hold values from 0 to 1, as said below
- mlp_gain: float32 [512], replicated, may hold values from 0.25 to 1.75
- w_up: bfloat16 [512, 2048], replicated, may hold values from -0.25 to 0.25
- w_down: bfloat16 [2048, 512], replicated, may hold values from -0.125 to 0.125
Outputs:
- result: bfloat16 [128, 1024, 512], P('lat', 'lon')
Inputs may be any that keep to these rules, and one draw needn't show every extreme that they name: `far_mask`: used slots come first in each block's list; every block uses at least 12 slots. `far_ids`: the tile of 16 x 64 tokens that one device holds is a grid of blocks; among all list slots of one such tile, used or not, the blocks of any one tile are named at most 6 times, and exactly 6 times for some tiles.
All inputs are finite; a program needn't handle non-finite values.
Results may differ from a plain program's by a relative error of at most 0.006.
The roundings to bfloat16 on the way count: a program that leaves them out, or rounds other values in their place, can miss the bound.
Values may be sent and summed in bfloat16 or wider, within the bound.
A program may use at most 128 MiB of HBM per device.

v0:
```python
import math

import jax
import jax.numpy as jnp
from jax import lax
from jax.sharding import PartitionSpec as P

BLK = 8
SUMROWS = 4
FAR = 48


eps = 1e-06


def padded_2(array, sides, width):
    for axis, dim in sides:
        size, length = (lax.axis_size(axis), array.shape[dim])
        up = [(i, (i + 1) % size) for i in range(size)]
        down = [(j, i) for i, j in up]
        last = lax.slice_in_dim(array, length - width, length, axis=dim)
        first = lax.slice_in_dim(array, 0, width, axis=dim)
        before = lax.ppermute(last, axis, up)
        after = lax.ppermute(first, axis, down)
        array = jnp.concatenate([before, array, after], axis=dim)
    return array


def rms_scale(values, scale_gain):
    wide = values.astype(jnp.float32)
    mean_square = jnp.mean(wide * wide, axis=-1, keepdims=True)
    return (wide * lax.rsqrt(mean_square + eps) * scale_gain).astype(jnp.bfloat16)


def project(values, weight):
    flat = values.reshape(-1, values.shape[-1])
    output = jnp.dot(flat, weight, preferred_element_type=jnp.float32).astype(jnp.bfloat16)
    return output.reshape(values.shape[:-1] + (weight.shape[1],))


def to_blocks(grid):
    row_count, col_count, feature = grid.shape
    shaped = grid.reshape(row_count // BLK, BLK, col_count // BLK, BLK, feature)
    return shaped.transpose(0, 2, 1, 3, 4).reshape(
        row_count // BLK, col_count // BLK, BLK * BLK, feature
    )


def local(
    tokens,
    norm_gain,
    w_query,
    w_key,
    w_value,
    w_out,
    pool_weight,
    head_scale,
    far_ids,
    far_mask,
    mlp_gain,
    w_up,
    w_down,
):
    tok_rows, tok_cols, feature = tokens.shape
    blk_rows = tok_rows // BLK
    blk_cols = tok_cols // BLK
    head_count = head_scale.shape[0]
    head_size = feature // head_count
    lat_count = lax.axis_size("lat")
    lon_count = lax.axis_size("lon")
    lat_index = lax.axis_index("lat")
    normed = rms_scale(tokens, norm_gain)
    query = project(normed, w_query)
    w_pair = jnp.concatenate([w_key, w_value], axis=1)
    paired = project(normed, w_pair)
    blocks = to_blocks(normed).reshape(blk_rows * blk_cols, BLK * BLK, feature)
    pooled = jnp.einsum("rt,btd->brd", pool_weight, blocks, preferred_element_type=jnp.float32)
    pooled = pooled.astype(jnp.bfloat16).reshape(blk_rows * blk_cols * SUMROWS, feature)
    padded = padded_2(paired, (("lat", 0), ("lon", 1)), BLK)
    global_cols = blk_cols * lon_count
    global_row = far_ids // global_cols
    global_col = far_ids % global_cols
    owner = global_row // blk_rows * lon_count + global_col // blk_cols
    inner_block = global_row % blk_rows * blk_cols + global_col % blk_cols
    gathered_index = owner * (blk_rows * blk_cols) + inner_block
    listed = gathered_index.reshape(-1)
    sub_rows = jnp.arange(SUMROWS, dtype=jnp.int32)
    listed_rows = (listed[:, None] * SUMROWS + sub_rows[None, :]).reshape(-1)
    summary = project(pooled, w_pair)
    every_pair = lax.all_gather(summary, ("lat", "lon"), axis=0, tiled=True)
    far_pair = jnp.take(every_pair, listed_rows, axis=0)
    far_pair = far_pair.reshape(blk_rows, blk_cols, FAR * SUMROWS, 2 * feature)
    place = jnp.arange(tok_rows + 2 * BLK, dtype=jnp.int32) + lat_index * tok_rows - BLK
    row_valid = (place >= 0) & (place < tok_rows * lat_count)
    query_blocks = to_blocks(query)
    score_scale = head_scale * (1.0 / math.sqrt(head_size))
    near_width = 3 * BLK * BLK

    def one_row(row_index):
        strip = lax.dynamic_slice_in_dim(padded, row_index * BLK, 3 * BLK, 0)
        shaped = strip.reshape(3 * BLK, blk_cols + 2, BLK, 2, head_count, head_size)
        key_grid = shaped[:, :, :, 0]
        value_grid = shaped[:, :, :, 1]
        row_query = lax.dynamic_index_in_dim(query_blocks, row_index, 0, keepdims=False)
        query_heads = row_query.reshape(blk_cols, BLK * BLK, head_count, head_size)
        far_rows = lax.dynamic_index_in_dim(far_pair, row_index, 0, keepdims=False)
        far_heads = far_rows.reshape(blk_cols, FAR * SUMROWS, 2, head_count, head_size)
        scores = []
        for offset in range(3):
            part_score = jnp.einsum(
                "cqhd,rckhd->chqrk",
                query_heads,
                key_grid[:, offset : offset + blk_cols],
                preferred_element_type=jnp.float32,
            )
            scores.append(part_score.reshape(blk_cols, head_count, BLK * BLK, near_width))
        scores.append(
            jnp.einsum(
                "cqhd,ckhd->chqk",
                query_heads,
                far_heads[:, :, 0],
                preferred_element_type=jnp.float32,
            )
        )
        score = jnp.concatenate(scores, axis=-1) * score_scale[None, :, None, None]
        strip_valid = lax.dynamic_slice_in_dim(row_valid, row_index * BLK, 3 * BLK, 0)
        near_valid = jnp.broadcast_to(strip_valid[:, None], (3 * BLK, BLK)).reshape(-1)
        row_mask = lax.dynamic_index_in_dim(far_mask, row_index, 0, keepdims=False)
        far_valid = jnp.repeat(row_mask > 0, SUMROWS, axis=1)
        near_all = jnp.concatenate([near_valid, near_valid, near_valid])
        valid = jnp.concatenate(
            [jnp.broadcast_to(near_all[None, :], (blk_cols, near_all.shape[0])), far_valid], axis=1
        )
        keep = valid[:, None, None, :]
        highest = jnp.max(jnp.where(keep, score, -1e30), axis=-1, keepdims=True)
        expo = jnp.exp(jnp.where(keep, score - highest, -1e30))
        weights = (expo / jnp.sum(expo, axis=-1, keepdims=True)).astype(jnp.bfloat16)
        mixed = jnp.einsum(
            "chqk,ckhd->cqhd",
            weights[..., 3 * near_width :],
            far_heads[:, :, 1],
            preferred_element_type=jnp.float32,
        )
        for offset in range(3):
            part_weight = weights[..., offset * near_width : (offset + 1) * near_width].reshape(
                blk_cols, head_count, BLK * BLK, 3 * BLK, BLK
            )
            mixed = mixed + jnp.einsum(
                "chqrk,rckhd->cqhd",
                part_weight,
                value_grid[:, offset : offset + blk_cols],
                preferred_element_type=jnp.float32,
            )
        return mixed.astype(jnp.bfloat16).reshape(blk_cols, BLK * BLK, feature)

    attended = lax.map(one_row, jnp.arange(blk_rows, dtype=jnp.int32))
    attn = (
        attended.reshape(blk_rows, blk_cols, BLK, BLK, feature)
        .transpose(0, 2, 1, 3, 4)
        .reshape(tok_rows * tok_cols, feature)
    )
    mixed = (
        tokens.reshape(-1, feature).astype(jnp.float32)
        + jnp.dot(attn, w_out, preferred_element_type=jnp.float32)
    ).astype(jnp.bfloat16)
    normed_two = rms_scale(mixed, mlp_gain)
    hidden = jax.nn.gelu(
        jnp.dot(normed_two, w_up, preferred_element_type=jnp.float32), approximate=True
    ).astype(jnp.bfloat16)
    result = (
        mixed.astype(jnp.float32) + jnp.dot(hidden, w_down, preferred_element_type=jnp.float32)
    ).astype(jnp.bfloat16)
    return result.reshape(tok_rows, tok_cols, feature)


def solution(mesh):
    return jax.shard_map(
        local,
        mesh=mesh,
        in_specs=(
            P("lat", "lon", None),
            P(),
            P(),
            P(),
            P(),
            P(),
            P(),
            P(),
            P("lat", "lon", None),
            P("lat", "lon", None),
            P(),
            P(),
            P(),
        ),
        out_specs=P("lat", "lon", None),
        check_vma=False,
    )
```

profile of v0, /device:TPU:1, one launch (start us, length us, event | category | flops | bytes accessed | tf_op | source)
XLA Modules:
  0.0 528.9 jit_solution(14609142763297510466)
XLA Ops:
  31.4 6.1 %collective-permute-done = bf16[8,64,1024]{2,1,0:T(8,128)(2,1)S(1)} collective-permute-done((bf16[8,64,1024]{2,1,0:T(8,128)(2,1)}, bf16[8,64,1024]{2,1,0:T(8,128)(2,1)S(1)}, u32[]{:S(2)}, u32[]{:S(2)}) %collective-permute-start) | collective-permute-done | bytes 1048608 | tf_op jit(solution)/shard_map/ppermute | solution.py:23
  46.6 13.8 %collective-permute-done.2 = bf16[32,8,1024]{2,1,0:T(8,128)(2,1)S(1)} collective-permute-done((bf16[32,8,1024]{2,1,0:T(8,128)(2,1)S(1)}, bf16[32,8,1024]{2,1,0:T(8,128)(2,1)S(1)}, u32[]{:S(2)}, u32[]{:S(2)}) %collective-permute-start.2) | collective-permute-done | bytes 524320 | tf_op jit(solution)/shard_map/ppermute | solution.py:23
  60.4 5.4 %pad_maximum_fusion = bf16[32,80,1024]{2,1,0:T(8,128)(2,1)} fusion(bf16[32,8,1024]{2,1,0:T(8,128)(2,1)S(1)} %collective-permute-done.3, bf16[8,64,1024]{2,1,0:T(8,128)(2,1)} %collective-permute-done.1, bf16[16,64,1024]{2,1,0:T(8,128)(2,1)S(1)} %bitcast.161, bf16[8,64,1024]{2,1,0:T(8,128)(2,1)S(1)} %collective-permute-done, ...), kind=kLoop, calls=%fused_computation.59 | loop fusion | flops 26214400 | bytes 10485760 | tf_op jit(solution)/shard_map/concatenate | solution.py:25
  65.8 38.2 %all-gather.2.cloned.1.call-done = bf16[8192,1024]{1,0:T(8,128)(2,1)} async-done(((bf16[64,1024]{1,0:T(8,128)(2,1)}), bf16[8192,1024]{1,0:T(8,128)(2,1)}) %all-gather.2.cloned.1.call-update) | async-done | bytes 16777232 | tf_op jit(solution)/shard_map/all_gather | solution.py:90
  104.0 23.9 %gather_fusion = bf16[3072,1024]{1,0:T(8,128)(2,1)} fusion(bf16[8192,1024]{1,0:T(8,128)(2,1)} %all-gather.2.cloned.1.call-done, s32[3072]{0:T(1024)S(1)} %broadcast_clamp_fusion), kind=kCustom, calls=%fused_computation | custom fusion | bytes 12595200 | tf_op jit(solution)/shard_map/jit(_take)/gather | solution.py:91
  128.0 11.1 %copy.73 = bf16[2,8,192,1024]{2,3,1,0:T(8,128)(2,1)} copy(bf16[2,8,192,1024]{3,2,1,0:T(8,128)(2,1)} %bitcast.159) | data formatting | bytes 12582912 | tf_op jit(solution)/shard_map/jit(_take)/gather | solution.py:91
  139.0 7.6 %broadcast_select_fusion = bf16[2,8,192,1024]{2,3,1,0:T(8,128)(2,1)} fusion(bf16[2,8,192,1024]{2,3,1,0:T(8,128)(2,1)} %copy.73, pred[2,8,192]{2,1,0:T(8,128)(4,1)S(1)} %compare_and_fusion), kind=kLoop, calls=%fused_computation.58 | loop fusion | flops 3145728 | bytes 12585984 | tf_op jit(solution)/shard_map/jit(_take)/select_n | solution.py:91
  146.6 364.2 %while.10 = (s32[]{:T(128)}, bf16[2,8,64,512]{3,2,1,0:T(8,128)(2,1)}, s32[2]{0:T(128)S(1)}, bf16[2,8,192,1024]{2,3,1,0:T(8,128)(2,1)}, pred[32]{0:T(512)(128)(4,...) while((s32[]{:T(128)}, ...), condition=%wide.region_4.5_spmd, body=%wide.region_1.4_spmd.sunk | while | flops 850403584 | bytes 223804016 | solution.py:156
  152.4 11.2 %reshape.180 = bf16[24,10,8,2,8,64]{5,4,3,2,1,0:T(8,128)(2,1)} reshape(bf16[24,80,1024]{2,1,0:T(8,128)(2,1)} %constant_dynamic-slice_fusion.11) | data formatting | bytes 7864320 | tf_op jit(solution)/shard_map/while/body/eval_jaxpr/reshape | solution.py:101
  163.6 5.6 %fusion.127 = (bf16[24,10,8,1,8,64]{5,4,3,2,1,0:T(8,128)(2,1)}, bf16[24,10,8,1,8,64]{5,4,3,2,1,0:T(8,128)(2,1)S(1)}) fusion(bf16[24,10,8,2,8,64]{5,4,3,2,1,0:T(8,128)(2,1)} %reshape.180), kind=kLoop, calls=%fused_computation.135.clone.1 | loop fusion | bytes 7864320 | tf_op jit(solution)/shard_map/while/body/eval_jaxpr/slice | solution.py:103
  187.0 6.8 %copy.162 = f32[8,8,64,192]{3,2,1,0:T(8,128)} copy(f32[8,8,64,192]{2,3,1,0:T(8,128)} %bitcast.150) | data formatting | bytes 6291456 | tf_op jit(solution)/shard_map/while/body/eval_jaxpr/reshape | solution.py:116
  201.6 6.3 %copy.164 = f32[8,8,64,192]{3,2,1,0:T(8,128)} copy(f32[8,8,64,192]{2,3,1,0:T(8,128)} %bitcast.151) | data formatting | bytes 6291456 | tf_op jit(solution)/shard_map/while/body/eval_jaxpr/reshape | solution.py:116
  215.5 6.3 %copy.166 = f32[8,8,64,192]{3,2,1,0:T(8,128)} copy(f32[8,8,64,192]{2,3,1,0:T(8,128)} %bitcast.152) | data formatting | bytes 6291456 | tf_op jit(solution)/shard_map/while/body/eval_jaxpr/reshape | solution.py:116
  227.0 41.4 %fusion.131 = (f32[8,8,64]{2,1,0:T(8,128)S(1)}, f32[8,8,64,768]{3,2,1,0:T(8,128)}) fusion(pred[8,768]{1,0:T(8,128)(4,1)S(1)} %pad_add_fusion.5, f32[8]{0:T(128)S(1)} %get-tuple-element.209, f32[8,8,64,192]{3,2,1,0:T(8,128)S(1)} %fusion.126, f32[8,8,64,192]{3,2,1,0:T(8,128)} %copy.162, f32[8,8,64,192]{3,2,1,0:T(8,128)} %copy.164, ...), kind=kOutput, calls=%fused_computation.137.clone.1 | output fusion | flops 37749504 | bytes 25188384 | tf_op jit(solution)/shard_map/while/body/eval_jaxpr/sub | solution.py:136
  268.4 8.0 %divide_convert_fusion.2 = bf16[8,8,64,768]{3,2,1,0:T(8,128)(2,1)} fusion(f32[8,8,64,768]{3,2,1,0:T(8,128)} %get-tuple-element.165, f32[8,8,64]{2,1,0:T(8,128)S(1)} %get-tuple-element.166), kind=kLoop, calls=%fused_computation.3.clone.1 | loop fusion | flops 6291456 | bytes 18890752 | tf_op jit(solution)/shard_map/while/body/eval_jaxpr/convert_element_type | solution.py:137
  276.5 7.2 %fusion.132 = (bf16[8,8,64,192]{3,2,1,0:T(8,128)(2,1)}, bf16[8,8,64,192]{3,2,1,0:T(8,128)(2,1)}, bf16[8,8,64,192]{3,2,1,0:T(8,128)(2,1)}) fusion(bf16[8,8,64,768]{3,2,1,0:T(8,128)(2,1)} %divide_convert_fusion.2), kind=kLoop, calls=%fused_computation.136.clone.1 | loop fusion | bytes 9437184 | tf_op jit(solution)/shard_map/while/body/eval_jaxpr/slice | solution.py:145
  288.1 8.2 %fusion.135 = f32[8,8,64,64,1]{3,2,4,1,0:T(8,128)} fusion(bf16[8,8,64,24,8]{2,4,3,1,0:T(8,128)(2,1)} %bitcast.156, bf16[24,10,8,1,8,64]{5,4,3,2,1,0:T(8,128)(2,1)} %get-tuple-element.168), kind=kOutput, calls=%fused_computation.24.clone.1 | convolution fusion | flops 100663296 | bytes 4587520 | tf_op jit(solution)/shard_map/while/body/eval_jaxpr/chqrk,rckhd->cqhd/dot_general | solution.py:148
  301.0 8.2 %fusion.134 = f32[8,8,64,64,1]{3,2,4,1,0:T(8,128)} fusion(bf16[8,8,64,24,8]{2,4,3,1,0:T(8,128)(2,1)} %bitcast.158, bf16[24,10,8,1,8,64]{5,4,3,2,1,0:T(8,128)(2,1)} %get-tuple-element.168), kind=kOutput, calls=%fused_computation.22.clone.1 | convolution fusion | flops 100663296 | bytes 4587520 | tf_op jit(solution)/shard_map/while/body/eval_jaxpr/chqrk,rckhd->cqhd/dot_general | solution.py:148
  313.7 7.0 %fusion.133 = f32[8,8,64,64,1]{3,2,4,1,0:T(8,128)S(1)} fusion(bf16[8,8,64,24,8]{2,4,3,1,0:T(8,128)(2,1)} %bitcast.157, bf16[24,10,8,1,8,64]{5,4,3,2,1,0:T(8,128)(2,1)} %get-tuple-element.168), kind=kOutput, calls=%fused_computation.20.clone.1 | convolution fusion | flops 100663296 | bytes 4587520 | tf_op jit(solution)/shard_map/while/body/eval_jaxpr/chqrk,rckhd->cqhd/dot_general | solution.py:148
  332.6 11.2 %reshape.180 = bf16[24,10,8,2,8,64]{5,4,3,2,1,0:T(8,128)(2,1)} reshape(bf16[24,80,1024]{2,1,0:T(8,128)(2,1)} %constant_dynamic-slice_fusion.11) | data formatting | bytes 7864320 | tf_op jit(solution)/shard_map/while/body/eval_jaxpr/reshape | solution.py:101
  343.8 5.6 %fusion.127 = (bf16[24,10,8,1,8,64]{5,4,3,2,1,0:T(8,128)(2,1)}, bf16[24,10,8,1,8,64]{5,4,3,2,1,0:T(8,128)(2,1)S(1)}) fusion(bf16[24,10,8,2,8,64]{5,4,3,2,1,0:T(8,128)(2,1)} %reshape.180), kind=kLoop, calls=%fused_computation.135.clone.1 | loop fusion | bytes 7864320 | tf_op jit(solution)/shard_map/while/body/eval_jaxpr/slice | solution.py:103
  349.5 4.9 copy.160
  367.3 6.5 %copy.162 = f32[8,8,64,192]{3,2,1,0:T(8,128)} copy(f32[8,8,64,192]{2,3,1,0:T(8,128)} %bitcast.150) | data formatting | bytes 6291456 | tf_op jit(solution)/shard_map/while/body/eval_jaxpr/reshape | solution.py:116
  381.5 6.3 %copy.164 = f32[8,8,64,192]{3,2,1,0:T(8,128)} copy(f32[8,8,64,192]{2,3,1,0:T(8,128)} %bitcast.151) | data formatting | bytes 6291456 | tf_op jit(solution)/shard_map/while/body/eval_jaxpr/reshape | solution.py:116
  395.5 6.3 %copy.166 = f32[8,8,64,192]{3,2,1,0:T(8,128)} copy(f32[8,8,64,192]{2,3,1,0:T(8,128)} %bitcast.152) | data formatting | bytes 6291456 | tf_op jit(solution)/shard_map/while/body/eval_jaxpr/reshape | solution.py:116
  407.0 41.5 %fusion.131 = (f32[8,8,64]{2,1,0:T(8,128)S(1)}, f32[8,8,64,768]{3,2,1,0:T(8,128)}) fusion(pred[8,768]{1,0:T(8,128)(4,1)S(1)} %pad_add_fusion.5, f32[8]{0:T(128)S(1)} %get-tuple-element.209, f32[8,8,64,192]{3,2,1,0:T(8,128)S(1)} %fusion.126, f32[8,8,64,192]{3,2,1,0:T(8,128)} %copy.162, f32[8,8,64,192]{3,2,1,0:T(8,128)} %copy.164, ...), kind=kOutput, calls=%fused_computation.137.clone.1 | output fusion | flops 37749504 | bytes 25188384 | tf_op jit(solution)/shard_map/while/body/eval_jaxpr/sub | solution.py:136
  448.4 8.0 %divide_convert_fusion.2 = bf16[8,8,64,768]{3,2,1,0:T(8,128)(2,1)} fusion(f32[8,8,64,768]{3,2,1,0:T(8,128)} %get-tuple-element.165, f32[8,8,64]{2,1,0:T(8,128)S(1)} %get-tuple-element.166), kind=kLoop, calls=%fused_computation.3.clone.1 | loop fusion | flops 6291456 | bytes 18890752 | tf_op jit(solution)/shard_map/while/body/eval_jaxpr/convert_element_type | solution.py:137
  456.5 7.2 %fusion.132 = (bf16[8,8,64,192]{3,2,1,0:T(8,128)(2,1)}, bf16[8,8,64,192]{3,2,1,0:T(8,128)(2,1)}, bf16[8,8,64,192]{3,2,1,0:T(8,128)(2,1)}) fusion(bf16[8,8,64,768]{3,2,1,0:T(8,128)(2,1)} %divide_convert_fusion.2), kind=kLoop, calls=%fused_computation.136.clone.1 | loop fusion | bytes 9437184 | tf_op jit(solution)/shard_map/while/body/eval_jaxpr/slice | solution.py:145
  468.1 8.2 %fusion.135 = f32[8,8,64,64,1]{3,2,4,1,0:T(8,128)} fusion(bf16[8,8,64,24,8]{2,4,3,1,0:T(8,128)(2,1)} %bitcast.156, bf16[24,10,8,1,8,64]{5,4,3,2,1,0:T(8,128)(2,1)} %get-tuple-element.168), kind=kOutput, calls=%fused_computation.24.clone.1 | convolution fusion | flops 100663296 | bytes 4587520 | tf_op jit(solution)/shard_map/while/body/eval_jaxpr/chqrk,rckhd->cqhd/dot_general | solution.py:148
  481.2 8.2 %fusion.134 = f32[8,8,64,64,1]{3,2,4,1,0:T(8,128)} fusion(bf16[8,8,64,24,8]{2,4,3,1,0:T(8,128)(2,1)} %bitcast.158, bf16[24,10,8,1,8,64]{5,4,3,2,1,0:T(8,128)(2,1)} %get-tuple-element.168), kind=kOutput, calls=%fused_computation.22.clone.1 | convolution fusion | flops 100663296 | bytes 4587520 | tf_op jit(solution)/shard_map/while/body/eval_jaxpr/chqrk,rckhd->cqhd/dot_general | solution.py:148
  493.9 7.0 %fusion.133 = f32[8,8,64,64,1]{3,2,4,1,0:T(8,128)S(1)} fusion(bf16[8,8,64,24,8]{2,4,3,1,0:T(8,128)(2,1)} %bitcast.157, bf16[24,10,8,1,8,64]{5,4,3,2,1,0:T(8,128)(2,1)} %get-tuple-element.168), kind=kOutput, calls=%fused_computation.20.clone.1 | convolution fusion | flops 100663296 | bytes 4587520 | tf_op jit(solution)/shard_map/while/body/eval_jaxpr/chqrk,rckhd->cqhd/dot_general | solution.py:148
  514.4 7.4 %fusion.43 = bf16[1024,512]{1,0:T(8,128)(2,1)} fusion(bf16[1024,512]{1,0:T(8,128)(2,1)S(1)} %get-tuple-element.101, bf16[2048,512]{1,0:T(8,128)(2,1)S(1)} %copy-done, bf16[512,2048]{1,0:T(8,128)(2,1)} %param.26, f32[512]{0:T(512)S(1)} %copy-done.13, f32[1024]{0:T(1024)S(1)} %add_rsqrt_fusion.1), kind=kOutput, calls=%fused_computation.67 | convolution fusion | flops 4317511680 | bytes 6297600 | tf_op jit(solution)/shard_map/dot_general | solution.py:171
  (138 shorter events, 154.9 us)
Async XLA Ops:
  6.5 507.8 %copy-start = (bf16[2048,512]{1,0:T(8,128)(2,1)S(1)}, bf16[2048,512]{1,0:T(8,128)(2,1)}, u32[]{:S(2)}) copy-start(bf16[2048,512]{1,0:T(8,128)(2,1)} %param.27) | copy-start | bytes 6291460
  6.5 5.2 copy-start.12
  6.5 97.5 %all-gather.2.cloned.1.call-start = ((), (), s32[]{:S(2)}) async-start(), calls=%async_computation | async-start | bytes 16908288 | tf_op jit(solution)/shard_map/all_gather | solution.py:90
  11.6 7.0 %copy-start.7 = (bf16[16,64,512]{2,1,0:T(8,128)(2,1)}, bf16[16,64,512]{2,1,0:T(8,128)(2,1)S(1)}, u32[]{:S(2)}) copy-start(bf16[16,64,512]{2,1,0:T(8,128)(2,1)S(1)} %multiply_convert_fusion) | copy-start | bytes 3145732
  18.6 1.3 copy-start.5
  19.9 4.6 copy-start.11
  21.5 16.0 %collective-permute-start = (bf16[8,64,1024]{2,1,0:T(8,128)(2,1)}, bf16[8,64,1024]{2,1,0:T(8,128)(2,1)S(1)}, u32[]{:S(2)}, u32[]{:S(2)}) collective-permute-start(bf16[8,64,1024]{2,1,0:T(8,128)(2,1)} %bitcast.38), channel_id=1, source_target_pairs={{0,16},{16,32},{32,48},{48,64},{64,80},{80,96},{96,112},{112,0},{1... | collective-permute-start | bytes 3145736 | tf_op jit(solution)/shard_map/ppermute | solution.py:23
  24.5 15.8 %collective-permute-start.1 = (bf16[8,64,1024]{2,1,0:T(8,128)(2,1)}, bf16[8,64,1024]{2,1,0:T(8,128)(2,1)}, u32[]{:S(2)}, u32[]{:S(2)}) collective-permute-start(bf16[8,64,1024]{2,1,0:T(8,128)(2,1)} %bitcast.40), channel_id=1, source_target_pairs={{16,0},{32,16},{48,32},{64,48},{80,64},{96,80},{112,96},{0,112},{1... | collective-permute-start | bytes 3145736 | tf_op jit(solution)/shard_map/ppermute | solution.py:24
  28.1 3.2 copy-start.14
  28.1 3.2 copy-start.10
  30.2 16.3 %copy-start.8 = (s32[2,8,192]{2,1,0:T(8,128)S(1)}, s32[2,8,192]{2,1,0:T(8,128)}, u32[]{:S(2)}) copy-start(s32[2,8,192]{2,1,0:T(8,128)} %copy.71) | copy-start | bytes 36868
  31.3 29.1 %copy-start.6 = (bf16[1024,1024]{1,0:T(8,128)(2,1)S(1)}, bf16[1024,1024]{1,0:T(8,128)(2,1)}, u32[]{:S(2)}) copy-start(bf16[1024,1024]{1,0:T(8,128)(2,1)} %copy-done.5) | copy-start | bytes 6291460
  41.5 18.9 %collective-permute-start.2 = (bf16[32,8,1024]{2,1,0:T(8,128)(2,1)S(1)}, bf16[32,8,1024]{2,1,0:T(8,128)(2,1)S(1)}, u32[]{:S(2)}, u32[]{:S(2)}) collective-permute-start(bf16[32,8,1024]{2,1,0:T(8,128)(2,1)S(1)} %get-tuple-element.96), channel_id=1, source_target_pairs={{0,1},{1,2},{2,3},{3,4},{4,5},{5,6},{6,7},{7,8},{8,9},{9,10},{10,1... | collective-permute-start | bytes 1572872 | tf_op jit(solution)/shard_map/ppermute | solution.py:23
  42.7 17.6 %collective-permute-start.3 = (bf16[32,8,1024]{2,1,0:T(8,128)(2,1)S(1)}, bf16[32,8,1024]{2,1,0:T(8,128)(2,1)S(1)}, u32[]{:S(2)}, u32[]{:S(2)}) collective-permute-start(bf16[32,8,1024]{2,1,0:T(8,128)(2,1)S(1)} %get-tuple-element.97), channel_id=1, source_target_pairs={{1,0},{2,1},{3,2},{4,3},{5,4},{6,5},{7,6},{8,7},{9,8},{10,9},{11,1... | collective-permute-start | bytes 1572872 | tf_op jit(solution)/shard_map/ppermute | solution.py:24
  139.0 7.6 %copy-start.9 = (s32[2,8,48]{2,1,0:T(8,128)S(1)}, s32[2,8,48]{2,1,0:T(8,128)}, u32[]{:S(2)}) copy-start(s32[2,8,48]{2,1,0:T(8,128)} %param.24) | copy-start | bytes 9220
  225.0 2.0 copy-start.1
  313.7 7.0 %copy-start.2 = (bf16[1,8,192,1024]{2,3,1,0:T(8,128)(2,1)S(1)}, bf16[1,8,192,1024]{2,3,1,0:T(8,128)(2,1)}, u32[]{:S(2)}) copy-start(bf16[1,8,192,1024]{2,3,1,0:T(8,128)(2,1)} %copy-done.1) | copy-start | bytes 9437188 | tf_op jit(solution)/shard_map/while
  313.7 7.0 %copy-start.3 = (f32[8,8,64,64,1]{3,2,4,1,0:T(8,128)S(1)}, f32[8,8,64,64,1]{3,2,4,1,0:T(8,128)}, u32[]{:S(2)}) copy-start(f32[8,8,64,64,1]{3,2,4,1,0:T(8,128)} %fusion.135) | copy-start | bytes 3145732 | tf_op jit(solution)/shard_map/while
  313.7 7.0 %copy-start.4 = (f32[8,8,64,64,1]{3,2,4,1,0:T(8,128)S(1)}, f32[8,8,64,64,1]{3,2,4,1,0:T(8,128)}, u32[]{:S(2)}) copy-start(f32[8,8,64,64,1]{3,2,4,1,0:T(8,128)} %fusion.134) | copy-start | bytes 3145732 | tf_op jit(solution)/shard_map/while
  404.9 2.0 copy-start.1
  493.9 7.0 %copy-start.2 = (bf16[1,8,192,1024]{2,3,1,0:T(8,128)(2,1)S(1)}, bf16[1,8,192,1024]{2,3,1,0:T(8,128)(2,1)}, u32[]{:S(2)}) copy-start(bf16[1,8,192,1024]{2,3,1,0:T(8,128)(2,1)} %copy-done.1) | copy-start | bytes 9437188 | tf_op jit(solution)/shard_map/while
  493.9 7.0 %copy-start.3 = (f32[8,8,64,64,1]{3,2,4,1,0:T(8,128)S(1)}, f32[8,8,64,64,1]{3,2,4,1,0:T(8,128)}, u32[]{:S(2)}) copy-start(f32[8,8,64,64,1]{3,2,4,1,0:T(8,128)} %fusion.135) | copy-start | bytes 3145732 | tf_op jit(solution)/shard_map/while
  493.9 7.0 %copy-start.4 = (f32[8,8,64,64,1]{3,2,4,1,0:T(8,128)S(1)}, f32[8,8,64,64,1]{3,2,4,1,0:T(8,128)}, u32[]{:S(2)}) copy-start(f32[8,8,64,64,1]{3,2,4,1,0:T(8,128)} %fusion.134) | copy-start | bytes 3145732 | tf_op jit(solution)/shard_map/while
  510.8 3.6 copy-start.13
Sparse Core Ops, SparseCore 0:
  16.2 87.7 all-gather.1
where the time goes:
time: 539 us; the launch traced here: 529 us
  local copies, waits for them, and re-layouts  227 us (42%)
  other arithmetic  117 us (22%)
  matrix products  92.3 us (17%)
  waiting for transfers between devices  60.9 us (11%)
  between operations  13.8 us (3%)
  loops' own time  9.32 us (2%)
  starting transfers between devices  8.05 us (1%)
    sub x2, other arithmetic, one_row(): expo = jnp.exp(jnp.where(keep, score - highest, -1e+30))  82.9 us
    dot_general x6, matrix products, one_row(): jnp.einsum('chqrk,rckhd->cqhd', part_weight, value_grid[:, offset:offset...  46.7 us
    slice x8, local copies, waits for them, and re-layouts, one_row(): weights[..., offset * near_width:(offset + 1) * near_width]  41.8 us
    reshape x6, local copies, waits for them, and re-layouts, one_row(): part_score.reshape(blk_cols, head_count, BLK * BLK, near_width)  38.6 us
    all_gather x1, waiting for transfers between devices, local(): every_pair = lax.all_gather(summary, ('lat', 'lon'), axis=0, tiled=True)  38.2 us
    gather x2, local copies, waits for them, and re-layouts, local(): far_pair = jnp.take(every_pair, listed_rows, axis=0)  35 us
    dot_general x6, local copies, waits for them, and re-layouts, one_row(): jnp.einsum('cqhd,rckhd->chqrk', query_heads, key_grid[:, offset:offset +...  24 us
    reshape x2, local copies, waits for them, and re-layouts, one_row(): shaped = strip.reshape(3 * BLK, blk_cols + 2, BLK, 2, head_count, head_size)  22.4 us
  transfers between devices with their start and end apart: 5, of which 4 were waited for; matrix products, arithmetic and copies ran while one was open for 3% of the time, Pallas kernels for 0%

commit v1 on v0

v1 whole, which is shorter than its diff:
```python
import functools
import math

import jax
import jax.numpy as jnp
from jax import lax
from jax.experimental import pallas as pl
from jax.experimental.pallas import tpu as pltpu
from jax.sharding import PartitionSpec as P

BLK = 8
TOK = BLK * BLK
SUMROWS = 4
FAR = 48
EPS = 1e-06
NEG = -1e30
LOG2E = 1.4426950408889634
F32 = jnp.float32
BF16 = jnp.bfloat16


def rms(wide, gain):
    mean_square = jnp.mean(wide * wide, axis=-1, keepdims=True)
    return (wide * lax.rsqrt(mean_square + EPS) * gain).astype(BF16)


def blocks_of_rows(rows):
    count = rows[0].shape[0] // BLK
    return [
        jnp.concatenate([row[j * BLK : (j + 1) * BLK] for row in rows], axis=0)
        for j in range(count)
    ]


def pool_kernel(tok_ref, gain_ref, pool_ref, out_ref):
    gain = gain_ref[...]
    blocks = blocks_of_rows([tok_ref[r].astype(F32) for r in range(BLK)])
    for j, block in enumerate(blocks):
        normed = rms(block, gain)
        pooled = jnp.dot(pool_ref[...], normed, preferred_element_type=F32)
        out_ref[j] = pooled.astype(BF16)


def pool_call(tokens, gain, pool_weight):
    rows, cols, feature = tokens.shape
    blk_rows, blk_cols = rows // BLK, cols // BLK
    return pl.pallas_call(
        pool_kernel,
        grid=(blk_rows,),
        in_specs=[
            pl.BlockSpec((BLK, cols, feature), lambda i: (i, 0, 0)),
            pl.BlockSpec((1, feature), lambda i: (0, 0)),
            pl.BlockSpec((SUMROWS, TOK), lambda i: (0, 0)),
        ],
        out_specs=pl.BlockSpec((blk_cols, SUMROWS, feature), lambda i: (i, 0, 0)),
        out_shape=jax.ShapeDtypeStruct((blk_rows * blk_cols, SUMROWS, feature), BF16),
        name="pool",
    )(tokens, gain.reshape(1, feature), pool_weight)


def qkv_kernel(
    tok_ref, up_ref, down_ref, left_ref, right_ref, ul_ref, ur_ref, dl_ref, dr_ref,
    gain_ref, wq_ref, wk_ref, wv_ref, q_ref, k_ref, v_ref, nb_ref,
):
    gain = gain_ref[...]
    for bi in range(4):
        if bi == 0:
            mid, lt, rt = up_ref, ul_ref, ur_ref
            base = 0
        elif bi == 3:
            mid, lt, rt = down_ref, dl_ref, dr_ref
            base = 0
        else:
            mid, lt, rt = tok_ref, left_ref, right_ref
            base = (bi - 1) * BLK
        left = blocks_of_rows([lt[base + r].astype(F32) for r in range(BLK)])
        middle = blocks_of_rows([mid[base + r].astype(F32) for r in range(BLK)])
        right = blocks_of_rows([rt[base + r].astype(F32) for r in range(BLK)])
        for bj, block in enumerate(left + middle + right):
            nb_ref[bj * TOK : (bj + 1) * TOK, :] = rms(block, gain)
        k_ref[bi] = jnp.dot(nb_ref[...], wk_ref[...], preferred_element_type=F32).astype(BF16)
        v_ref[bi] = jnp.dot(nb_ref[...], wv_ref[...], preferred_element_type=F32).astype(BF16)
        if bi in (1, 2):
            local = nb_ref[TOK : TOK + 8 * TOK, :]
            q_ref[bi - 1] = jnp.dot(local, wq_ref[...], preferred_element_type=F32).astype(BF16)


def qkv_call(tokens, halos, gain, w_query, w_key, w_value):
    rows, cols, feature = tokens.shape
    blk_cols = cols // BLK
    wide = (blk_cols + 2) * TOK
    return pl.pallas_call(
        qkv_kernel,
        out_shape=(
            jax.ShapeDtypeStruct((2, blk_cols * TOK, feature), BF16),
            jax.ShapeDtypeStruct((4, wide, feature), BF16),
            jax.ShapeDtypeStruct((4, wide, feature), BF16),
        ),
        scratch_shapes=[pltpu.VMEM((wide, feature), BF16)],
        compiler_params=pltpu.CompilerParams(vmem_limit_bytes=40 << 20),
        cost_estimate=pl.CostEstimate(
            flops=2 * (2 * 4 * wide + rows * cols) * feature * feature,
            bytes_accessed=8 << 20,
            transcendentals=0,
        ),
        name="qkv",
    )(tokens, *halos, gain.reshape(1, feature), w_query, w_key, w_value)


def gelu(x):
    return jax.nn.gelu(x, approximate=True)


def main_kernel(
    idx_ref, scale_ref, bias_ref, q_ref, k_ref, v_ref, pooled_ref, wk_ref, wv_ref, mgain_ref,
    tok_hbm, wout_hbm, wup_hbm, wdown_hbm,
    out_ref,
    far_ref, kf_ref, vf_ref, attn_ref, tok_ref, wout_ref, wup_ref, wdown_ref, sems,
):
    copies = [
        pltpu.make_async_copy(src, dst, sems.at[n])
        for n, (src, dst) in enumerate(
            ((tok_hbm, tok_ref), (wout_hbm, wout_ref), (wup_hbm, wup_ref), (wdown_hbm, wdown_ref))
        )
    ]
    for copy in copies:
        copy.start()
    lane_head = lax.broadcasted_iota(jnp.int32, (TOK, 256), 1) // TOK

    for i in range(2):
        order = (1, 2, 0) if i == 0 else (0, 1, 2)

        def one_block(j, carry):
            b = i * 8 + j
            for s in range(FAR):
                far_ref[s * SUMROWS : (s + 1) * SUMROWS, :] = pooled_ref[idx_ref[b, s]]
            far = far_ref[...]
            kf_ref[...] = jnp.dot(far, wk_ref[...], preferred_element_type=F32).astype(BF16)
            vf_ref[...] = jnp.dot(far, wv_ref[...], preferred_element_type=F32).astype(BF16)
            start = pl.multiple_of(j * TOK, TOK)
            bias = bias_ref[b]
            for g in range(2):
                feats = slice(g * 256, (g + 1) * 256)
                query = q_ref[i, pl.ds(start, TOK), feats]
                stacked = jnp.concatenate(
                    [jnp.where(lane_head == h, query, jnp.zeros_like(query)) for h in range(4)], axis=0
                )
                keys = jnp.concatenate(
                    [k_ref[i + d, pl.ds(start, 3 * TOK), feats] for d in order] + [kf_ref[:, feats]], axis=0
                )
                values = jnp.concatenate(
                    [v_ref[i + d, pl.ds(start, 3 * TOK), feats] for d in order] + [vf_ref[:, feats]], axis=0
                )
                score = lax.dot_general(
                    stacked, keys, (((1,), (1,)), ((), ())), preferred_element_type=F32
                )
                weights = []
                for h in range(4):
                    part = score[h * TOK : (h + 1) * TOK]
                    part = jnp.concatenate([part[:, :384], part[:, 384:] + bias], axis=1)
                    highest = jnp.max(part, axis=-1, keepdims=True)
                    expo = jnp.exp2((part - highest) * scale_ref[0, g * 4 + h])
                    total = jnp.sum(expo, axis=-1, keepdims=True)
                    weights.append((expo * (1.0 / total)).astype(BF16))
                weight = jnp.concatenate(weights, axis=0)
                full = jnp.dot(weight, values, preferred_element_type=F32)
                picked = jnp.zeros((TOK, 256), F32)
                for h in range(4):
                    picked = jnp.where(lane_head == h, full[h * TOK : (h + 1) * TOK], picked)
                attn_ref[i, pl.ds(start, TOK), feats] = picked.astype(BF16)
            return carry

        lax.fori_loop(0, 8, one_block, 0)

    for copy in copies:
        copy.wait()
    mgain = mgain_ref[...]
    for i in range(2):
        token_blocks = blocks_of_rows([tok_ref[i * BLK + r].astype(F32) for r in range(BLK)])
        for half in range(2):
            rows = slice(half * 256, (half + 1) * 256)
            token = jnp.concatenate(token_blocks[half * 4 : half * 4 + 4], axis=0)
            mixed = (
                token + jnp.dot(attn_ref[i, rows, :], wout_ref[...], preferred_element_type=F32)
            ).astype(BF16)
            wide = mixed.astype(F32)
            normed = rms(wide, mgain)
            acc = wide
            for f in range(4):
                part = slice(f * 512, (f + 1) * 512)
                hidden = gelu(
                    jnp.dot(normed, wup_ref[:, part], preferred_element_type=F32)
                ).astype(BF16)
                acc = acc + jnp.dot(hidden, wdown_ref[part, :], preferred_element_type=F32)
            for r in range(BLK):
                row = jnp.concatenate(
                    [acc[j * TOK + r * BLK : j * TOK + (r + 1) * BLK] for j in range(4)], axis=0
                )
                out_ref[i * BLK + r, half * 32 : (half + 1) * 32, :] = row.astype(BF16)


def main_call(idx, scale, bias, q, k, v, pooled, w_key, w_value, mlp_gain, tokens, w_out, w_up, w_down):
    rows, cols, feature = tokens.shape
    vmem = pl.BlockSpec(memory_space=pltpu.VMEM)
    smem = pl.BlockSpec(memory_space=pltpu.SMEM)
    hbm = pl.BlockSpec(memory_space=pl.ANY)
    return pl.pallas_call(
        main_kernel,
        out_shape=jax.ShapeDtypeStruct(tokens.shape, BF16),
        in_specs=[smem, smem] + [vmem] * 8 + [hbm] * 4,
        out_specs=vmem,
        scratch_shapes=[
            pltpu.VMEM((FAR * SUMROWS, feature), BF16),
            pltpu.VMEM((FAR * SUMROWS, feature), BF16),
            pltpu.VMEM((FAR * SUMROWS, feature), BF16),
            pltpu.VMEM((2, 8 * TOK, feature), BF16),
            pltpu.VMEM(tokens.shape, BF16),
            pltpu.VMEM(w_out.shape, BF16),
            pltpu.VMEM(w_up.shape, BF16),
            pltpu.VMEM(w_down.shape, BF16),
            pltpu.SemaphoreType.DMA((4,)),
        ],
        compiler_params=pltpu.CompilerParams(vmem_limit_bytes=56 << 20),
        cost_estimate=pl.CostEstimate(
            flops=20_000_000_000, bytes_accessed=24 << 20, transcendentals=6_000_000
        ),
        name="main",
    )(idx, scale, bias, q, k, v, pooled, w_key, w_value, mlp_gain.reshape(1, feature), tokens, w_out, w_up, w_down)


def shifted(value, lat_step, lon_step):
    lat_count, lon_count = lax.axis_size("lat"), lax.axis_size("lon")
    pairs = []
    for a in range(lat_count):
        for o in range(lon_count):
            ta, to = a + lat_step, (o + lon_step) % lon_count
            if 0 <= ta < lat_count:
                pairs.append((a * lon_count + o, ta * lon_count + to))
    return lax.ppermute(value, ("lat", "lon"), pairs)


def local(
    tokens, norm_gain, w_query, w_key, w_value, w_out, pool_weight, head_scale,
    far_ids, far_mask, mlp_gain, w_up, w_down,
):
    rows, cols, feature = tokens.shape
    blk_rows, blk_cols = rows // BLK, cols // BLK
    heads = head_scale.shape[0]
    lat_count, lon_count = lax.axis_size("lat"), lax.axis_size("lon")
    lat_index = lax.axis_index("lat")
    pooled = pool_call(tokens, norm_gain, pool_weight)
    every = lax.all_gather(pooled, ("lat", "lon"), axis=0, tiled=True)
    up = shifted(tokens[rows - BLK :], 1, 0)
    down = shifted(tokens[:BLK], -1, 0)
    left = shifted(tokens[:, cols - BLK :], 0, 1)
    right = shifted(tokens[:, :BLK], 0, -1)
    ul = shifted(tokens[rows - BLK :, cols - BLK :], 1, 1)
    ur = shifted(tokens[rows - BLK :, :BLK], 1, -1)
    dl = shifted(tokens[:BLK, cols - BLK :], -1, 1)
    dr = shifted(tokens[:BLK, :BLK], -1, -1)
    q, k, v = qkv_call(
        tokens, (up, down, left, right, ul, ur, dl, dr), norm_gain, w_query, w_key, w_value
    )
    global_cols = blk_cols * lon_count
    global_row = far_ids // global_cols
    global_col = far_ids % global_cols
    owner = global_row // blk_rows * lon_count + global_col // blk_cols
    inner_block = global_row % blk_rows * blk_cols + global_col % blk_cols
    idx = (owner * (blk_rows * blk_cols) + inner_block).reshape(blk_rows * blk_cols, FAR)
    far_valid = jnp.repeat(far_mask.reshape(blk_rows * blk_cols, FAR) > 0, SUMROWS, axis=1)
    block_row = jnp.arange(blk_rows * blk_cols) // blk_cols
    edge_ok = jnp.where(block_row == 0, lat_index > 0, lat_index < lat_count - 1)
    valid = jnp.concatenate(
        [jnp.broadcast_to(edge_ok[:, None], (blk_rows * blk_cols, 3 * TOK)), far_valid], axis=1
    )
    bias = jnp.where(valid, 0.0, NEG).astype(F32)[:, None, :]
    scale = (head_scale * (LOG2E / math.sqrt(feature // heads))).reshape(1, heads)
    return main_call(
        idx, scale, bias, q, k, v, every, w_key, w_value, mlp_gain, tokens, w_out, w_up, w_down
    )


def solution(mesh):
    return jax.shard_map(
        local,
        mesh=mesh,
        in_specs=(
            P("lat", "lon", None),
            P(), P(), P(), P(), P(), P(), P(),
            P("lat", "lon", None),
            P("lat", "lon", None),
            P(), P(), P(),
        ),
        out_specs=P("lat", "lon", None),
        check_vma=False,
    )
```

time: 539 us -> 129 us (0.24); the launches traced: 529 us -> 128 us
  local copies, waits for them, and re-layouts: 227 us -> 11.8 us
  other arithmetic: 117 us -> 3.23 us
  matrix products: 92.3 us -> 0 us
  Pallas kernels: 0 us -> 43.8 us
  waiting for transfers between devices: 60.9 us -> 29.8 us
  starting transfers between devices: 8.05 us -> 25.9 us
  loops' own time: 9.32 us -> 0 us
    dot_general x22 -> x0, matrix products: 92.3 us -> none  [the longest x6 46.7 us: one_row(): jnp.einsum('chqrk,rckhd->cqhd', part_weight, value_grid[:, offset:offset...]
    sub x2 -> x0, other arithmetic: 82.9 us -> none  [one_row(): expo = jnp.exp(jnp.where(keep, score - highest, -1e+30))]
    reshape x15 -> x0, local copies, waits for them, and re-layouts: 64.7 us -> none  [the longest x6 38.6 us: one_row(): part_score.reshape(blk_cols, head_count, BLK * BLK, near_width)]
    slice x11 -> x3, local copies, waits for them, and re-layouts: 54.7 us -> 4.6 us  [the longest x1 2.28 us: local(): down = shifted(tokens[:BLK], -1, 0)]
    pallas_call x0 -> x3, Pallas kernels: none -> 43.8 us  [the longest x1 36.7 us: main_call(): pl.pallas_call(main_kernel, out_shape=jax.ShapeDtypeStruct(tokens.shape,...]
    gather x2 -> x0, local copies, waits for them, and re-layouts: 35 us -> none  [local(): far_pair = jnp.take(every_pair, listed_rows, axis=0)]
    dot_general x6 -> x0, local copies, waits for them, and re-layouts: 24 us -> none  [one_row(): jnp.einsum('cqhd,rckhd->chqrk', query_heads, key_grid[:, offset:offset +...]
    dynamic_slice x14 -> x0, local copies, waits for them, and re-layouts: 19.4 us -> none  [the longest x2 9.25 us: one_row(): strip = lax.dynamic_slice_in_dim(padded, row_index * BLK, 3 * BLK, 0)]
  transfers between devices with their start and end apart: 5 -> 9, of which waited for: 4 -> 2; matrix products, arithmetic and copies ran while one was open for 3% -> 8% of each run, Pallas kernels for 0% -> 4%
where the time goes in v1:
time: 129 us; the launch traced here: 128 us
  Pallas kernels  43.8 us (34%)
  waiting for transfers between devices  29.8 us (23%)
  starting transfers between devices  25.9 us (20%)
  between operations  13.6 us (11%)
  local copies, waits for them, and re-layouts  11.8 us (9%)
  other arithmetic  3.23 us (3%)
    pallas_call x1, Pallas kernels, main_call(): pl.pallas_call(main_kernel, out_shape=jax.ShapeDtypeStruct(tokens.shape,...  36.7 us
    all_gather x1, waiting for transfers between devices, local(): every = lax.all_gather(pooled, ('lat', 'lon'), axis=0, tiled=True)  26.1 us
    ppermute x8, starting transfers between devices, shifted(): return lax.ppermute(value, ('lat', 'lon'), pairs)  25.8 us
    pallas_call x1, Pallas kernels, qkv_call(): pl.pallas_call(qkv_kernel, out_shape=(jax.ShapeDtypeStruct((2, blk_cols *...  4.64 us
    unnamed x22, local copies, waits for them, and re-layouts  4.2 us
    ppermute x8, waiting for transfers between devices, shifted(): return lax.ppermute(value, ('lat', 'lon'), pairs)  3.77 us
  transfers between devices with their start and end apart: 9, of which 2 were waited for; matrix products, arithmetic and copies ran while one was open for 8% of the time, Pallas kernels for 4%

profile of v1, /device:TPU:1, one launch (start us, length us, event | category | flops | bytes accessed | tf_op | source)
XLA Modules:
  0.0 128.2 jit_solution(365118623755918513)
XLA Ops:
  6.6 0.0 copy-start.3
  6.6 0.0 copy-start.4
  6.6 0.0 all-gather.2.cloned.1.call-start
  6.6 2.5 %pool.1 = bf16[16,4,512]{2,1,0:T(4,128)(2,1)} custom-call(bf16[16,64,512]{2,1,0:T(8,128)(2,1)} %tok_hbm.1, f32[1,512]{1,0:T(1,128)} %bitcast.9, bf16[4,64]{1,0:T(4,128)(2,1)} %pool_ref.1), custom_call_target="tpu_custom_call" | custom-call | tf_op jit(solution)/shard_map/pool/pallas_call | solution.py:47
  9.1 0.0 all-gather.2.cloned.1.call-update
  9.1 1.6 %fusion.17 = (bf16[8,8,512]{2,1,0:T(8,128)(2,1)}, bf16[8,8,512]{2,1,0:T(8,128)(2,1)}, bf16[8,8,512]{2,1,0:T(8,128)(2,1)S(1)}, bf16[8,8,512]{2,1,0:T(8,128)(2,1)S(1)}) fusion(bf16[16,64,512]{2,1,0:T(8,128)(2,1)} %tok_hbm.1), kind=kLoop, calls=%fused_computation.43 | loop fusion | bytes 524288 | tf_op jit(solution)/shard_map/slice | solution.py:260
  10.7 5.8 %collective-permute-start.4 = (bf16[8,8,512]{2,1,0:T(8,128)(2,1)S(1)}, bf16[8,8,512]{2,1,0:T(8,128)(2,1)S(1)}, u32[]{:S(2)}, u32[]{:S(2)}) collective-permute-start(bf16[8,8,512]{2,1,0:T(8,128)(2,1)S(1)} %get-tuple-element.14), channel_id=1, source_target_pairs={{0,17},{1,18},{2,19},{3,20},{4,21},{5,22},{6,23},{7,24},{8,25},{9,... | collective-permute-start | bytes 196616 | tf_op jit(solution)/shard_map/ppermute | solution.py:239
  16.6 5.6 %collective-permute-start.5 = (bf16[8,8,512]{2,1,0:T(8,128)(2,1)S(1)}, bf16[8,8,512]{2,1,0:T(8,128)(2,1)S(1)}, u32[]{:S(2)}, u32[]{:S(2)}) collective-permute-start(bf16[8,8,512]{2,1,0:T(8,128)(2,1)S(1)} %get-tuple-element.13), channel_id=1, source_target_pairs={{0,31},{1,16},{2,17},{3,18},{4,19},{5,20},{6,21},{7,22},{8,23},{9,... | collective-permute-start | bytes 196616 | tf_op jit(solution)/shard_map/ppermute | solution.py:239
  22.2 1.9 %collective-permute-start.6 = (bf16[8,8,512]{2,1,0:T(8,128)(2,1)}, bf16[8,8,512]{2,1,0:T(8,128)(2,1)}, u32[]{:S(2)}, u32[]{:S(2)}) collective-permute-start(bf16[8,8,512]{2,1,0:T(8,128)(2,1)} %get-tuple-element.12), channel_id=1, source_target_pairs={{16,1},{17,2},{18,3},{19,4},{20,5},{21,6},{22,7},{23,8},{24,9},{25... | collective-permute-start | bytes 196616 | tf_op jit(solution)/shard_map/ppermute | solution.py:239
  24.2 2.3 %fusion.19 = (bf16[8,64,512]{2,1,0:T(8,128)(2,1)}, bf16[8,64,512]{2,1,0:T(8,128)(2,1)}) fusion(bf16[16,64,512]{2,1,0:T(8,128)(2,1)} %tok_hbm.1), kind=kLoop, calls=%fused_computation.45 | loop fusion | bytes 2097152 | tf_op jit(solution)/shard_map/slice | solution.py:254
  26.5 3.7 %collective-permute-start = (bf16[8,64,512]{2,1,0:T(8,128)(2,1)}, bf16[8,64,512]{2,1,0:T(8,128)(2,1)S(1)}, u32[]{:S(2)}, u32[]{:S(2)}) collective-permute-start(bf16[8,64,512]{2,1,0:T(8,128)(2,1)} %get-tuple-element.18), channel_id=1, source_target_pairs={{0,16},{1,17},{2,18},{3,19},{4,20},{5,21},{6,22},{7,23},{8,24},{9,... | collective-permute-start | bytes 1572872 | tf_op jit(solution)/shard_map/ppermute | solution.py:239
  30.1 1.9 %collective-permute-start.1 = (bf16[8,64,512]{2,1,0:T(8,128)(2,1)}, bf16[8,64,512]{2,1,0:T(8,128)(2,1)}, u32[]{:S(2)}, u32[]{:S(2)}) collective-permute-start(bf16[8,64,512]{2,1,0:T(8,128)(2,1)} %get-tuple-element.17), channel_id=1, source_target_pairs={{16,0},{17,1},{18,2},{19,3},{20,4},{21,5},{22,6},{23,7},{24,8},{25... | collective-permute-start | bytes 1572872 | tf_op jit(solution)/shard_map/ppermute | solution.py:239
  32.1 0.6 fusion.4.idx_ref
  32.7 0.7 fusion.18
  33.4 0.6 multiply_bitcast_fusion.scale_ref
  34.0 0.0 collective-permute-done.4.ul_ref
  34.0 4.8 %collective-permute-start.3 = (bf16[16,8,512]{2,1,0:T(8,128)(2,1)}, bf16[16,8,512]{2,1,0:T(8,128)(2,1)S(1)}, u32[]{:S(2)}, u32[]{:S(2)}) collective-permute-start(bf16[16,8,512]{2,1,0:T(8,128)(2,1)} %get-tuple-element.15), channel_id=1, source_target_pairs={{0,15},{1,0},{2,1},{3,2},{4,3},{5,4},{6,5},{7,6},{8,7},{9,8},{10,9... | collective-permute-start | bytes 393224 | tf_op jit(solution)/shard_map/ppermute | solution.py:239
  38.8 0.6 compare_select_fusion
  39.4 0.1 copy.19
  39.5 0.6 broadcast_in_dim.29
  40.1 1.5 %copy.20 = pred[16,1,192]{2,1,0:T(4,128)(4,1)} copy(pred[16,1,192]{0,2,1:T(8,128)(4,1)} %bitcast.11) | data formatting | bytes 6144 | tf_op jit(solution)/shard_map/concatenate | solution.py:273
  41.6 2.1 %collective-permute-start.7 = (bf16[8,8,512]{2,1,0:T(8,128)(2,1)}, bf16[8,8,512]{2,1,0:T(8,128)(2,1)S(1)}, u32[]{:S(2)}, u32[]{:S(2)}) collective-permute-start(bf16[8,8,512]{2,1,0:T(8,128)(2,1)} %get-tuple-element.11), channel_id=1, source_target_pairs={{16,15},{17,0},{18,1},{19,2},{20,3},{21,4},{22,5},{23,6},{24,7},{2... | collective-permute-start | bytes 196616 | tf_op jit(solution)/shard_map/ppermute | solution.py:239
  43.7 0.8 broadcast_in_dim.28
  44.5 1.4 %add_select_fusion.bias_ref = f32[16,1,384]{2,1,0:T(1,128)} fusion(pred[16,1,192]{2,1,0:T(4,128)(4,1)} %copy.20, pred[16,1,192]{2,1,0:T(4,128)(4,1)S(1)} %broadcast_in_dim.28), kind=kLoop, calls=%fused_computation | loop fusion | flops 12288 | bytes 30720 | tf_op jit(solution)/shard_map/jit(_where)/select_n | solution.py:276
  45.9 3.7 %collective-permute-done.7.dr_ref = bf16[8,8,512]{2,1,0:T(8,128)(2,1)S(1)} collective-permute-done((bf16[8,8,512]{2,1,0:T(8,128)(2,1)}, bf16[8,8,512]{2,1,0:T(8,128)(2,1)S(1)}, u32[]{:S(2)}, u32[]{:S(2)}) %collective-permute-start.7) | collective-permute-done | bytes 65568 | tf_op jit(solution)/shard_map/ppermute | solution.py:239
  49.7 0.0 collective-permute-done.up_ref
  49.7 4.6 %qkv.1 = (bf16[2,512,512]{2,1,0:T(8,128)(2,1)S(1)}, bf16[4,640,512]{2,1,0:T(8,128)(2,1)S(1)}, bf16[4,640,512]{2,1,0:T(8,128)(2,1)S(1)}) custom-call(bf16[16,64,512]{2,1,0:T(8,128)(2,1)S(1)} %copy-done, bf16[8,64,512]{2,1,0:T(8,128)(2,1)S(1)} %collective-permute-done.up_ref, bf16[8,64,512]{2,1,0:T(8,128)(2,1)} %collective-permute-done.1.down_ref, ...), custom_call_target="tpu_custom_call" | custom-call | flops 3221225472 | bytes 8388608 | tf_op jit(solution)/shard_map/qkv/pallas_call | solution.py:92
  54.4 1.6 %copy-done.5 = bf16[4,640,512]{2,1,0:T(8,128)(2,1)} copy-done((bf16[4,640,512]{2,1,0:T(8,128)(2,1)}, bf16[4,640,512]{2,1,0:T(8,128)(2,1)S(1)}, u32[]{:S(2)}) %copy-start.5) | copy-done | bytes 2621464
  55.9 1.6 %copy-done.6 = bf16[4,640,512]{2,1,0:T(8,128)(2,1)} copy-done((bf16[4,640,512]{2,1,0:T(8,128)(2,1)}, bf16[4,640,512]{2,1,0:T(8,128)(2,1)S(1)}, u32[]{:S(2)}) %copy-start.6) | copy-done | bytes 2621464
  57.5 1.0 copy-done.7
  58.5 26.1 %all-gather.2.cloned.1.call-done.pooled_ref = bf16[2048,4,512]{2,1,0:T(4,128)(2,1)} async-done(((bf16[16,4,512]{2,1,0:T(4,128)(2,1)}), bf16[2048,4,512]{2,1,0:T(4,128)(2,1)}) %all-gather.2.cloned.1.call-update) | async-done | bytes 8388624 | tf_op jit(solution)/shard_map/all_gather | solution.py:252
  84.6 36.7 %main.1 = bf16[16,64,512]{2,1,0:T(8,128)(2,1)} custom-call(s32[16,48]{1,0:T(8,128)} %fusion.4.idx_ref, f32[1,8]{1,0:T(1,128)} %multiply_bitcast_fusion.scale_ref, f32[16,1,384]{2,1,0:T(1,128)} %add_select_fusion.bias_ref, bf16[2,512,512]{2,1,0:T(8,128)(2,1)} %copy-done.7, bf16[4,640,512]{2,1,0:T(8,128)(2,1)} %copy-done.5, bf16[4,640,512]{2,1,0:T(8,128)(2,1)} %copy-done.6, ...), custom_call_target="tpu_custom_call" | custom-call | flops 20000000000 | bytes 25165824 | tf_op jit(solution)/shard_map/main/pallas_call | solution.py:207
  (24 shorter events, 0.1 us)
Async XLA Ops:
  6.5 26.1 %copy-start = (bf16[16,64,512]{2,1,0:T(8,128)(2,1)S(1)}, bf16[16,64,512]{2,1,0:T(8,128)(2,1)}, u32[]{:S(2)}) copy-start(bf16[16,64,512]{2,1,0:T(8,128)(2,1)} %tok_hbm.1) | copy-start | bytes 3145732
  6.5 43.1 %copy-start.1 = (f32[512]{0:T(512)S(1)}, f32[512]{0:T(512)}, u32[]{:S(2)}) copy-start(f32[512]{0:T(512)} %param.14) | copy-start | bytes 6148
  6.5 25.5 %copy-start.9 = (s32[2,8,48]{2,1,0:T(8,128)S(1)}, s32[2,8,48]{2,1,0:T(8,128)}, u32[]{:S(2)}) copy-start(s32[2,8,48]{2,1,0:T(8,128)} %param.21) | copy-start | bytes 9220
  6.5 26.9 %copy-start.8 = (s32[2,8,48]{2,1,0:T(8,128)S(1)}, s32[2,8,48]{2,1,0:T(8,128)}, u32[]{:S(2)}) copy-start(s32[2,8,48]{2,1,0:T(8,128)} %param.22) | copy-start | bytes 9220
  6.5 26.9 %copy-start.10 = (f32[8]{0:T(128)S(1)}, f32[8]{0:T(128)}, u32[]{:S(2)}) copy-start(f32[8]{0:T(128)} %param.20) | copy-start | bytes 100
  6.5 43.1 %copy-start.2 = (bf16[512,512]{1,0:T(8,128)(2,1)S(1)}, bf16[512,512]{1,0:T(8,128)(2,1)}, u32[]{:S(2)}) copy-start(bf16[512,512]{1,0:T(8,128)(2,1)} %wq_ref.1) | copy-start | bytes 1572868
  6.6 43.1 %copy-start.3 = (bf16[512,512]{1,0:T(8,128)(2,1)S(1)}, bf16[512,512]{1,0:T(8,128)(2,1)}, u32[]{:S(2)}) copy-start(bf16[512,512]{1,0:T(8,128)(2,1)} %wk_ref.3) | copy-start | bytes 1572868
  6.6 43.1 %copy-start.4 = (bf16[512,512]{1,0:T(8,128)(2,1)S(1)}, bf16[512,512]{1,0:T(8,128)(2,1)}, u32[]{:S(2)}) copy-start(bf16[512,512]{1,0:T(8,128)(2,1)} %wv_ref.3) | copy-start | bytes 1572868
  6.6 78.0 %all-gather.2.cloned.1.call-start = ((), (), s32[]{:S(2)}) async-start(), calls=%async_computation | async-start | bytes 8454144 | tf_op jit(solution)/shard_map/all_gather | solution.py:252
  10.7 23.3 %collective-permute-start.4 = (bf16[8,8,512]{2,1,0:T(8,128)(2,1)S(1)}, bf16[8,8,512]{2,1,0:T(8,128)(2,1)S(1)}, u32[]{:S(2)}, u32[]{:S(2)}) collective-permute-start(bf16[8,8,512]{2,1,0:T(8,128)(2,1)S(1)} %get-tuple-element.14), channel_id=1, source_target_pairs={{0,17},{1,18},{2,19},{3,20},{4,21},{5,22},{6,23},{7,24},{8,25},{9,... | collective-permute-start | bytes 196616 | tf_op jit(solution)/shard_map/ppermute | solution.py:239
  16.6 17.4 %collective-permute-start.5 = (bf16[8,8,512]{2,1,0:T(8,128)(2,1)S(1)}, bf16[8,8,512]{2,1,0:T(8,128)(2,1)S(1)}, u32[]{:S(2)}, u32[]{:S(2)}) collective-permute-start(bf16[8,8,512]{2,1,0:T(8,128)(2,1)S(1)} %get-tuple-element.13), channel_id=1, source_target_pairs={{0,31},{1,16},{2,17},{3,18},{4,19},{5,20},{6,21},{7,22},{8,23},{9,... | collective-permute-start | bytes 196616 | tf_op jit(solution)/shard_map/ppermute | solution.py:239
  22.2 19.4 %collective-permute-start.6 = (bf16[8,8,512]{2,1,0:T(8,128)(2,1)}, bf16[8,8,512]{2,1,0:T(8,128)(2,1)}, u32[]{:S(2)}, u32[]{:S(2)}) collective-permute-start(bf16[8,8,512]{2,1,0:T(8,128)(2,1)} %get-tuple-element.12), channel_id=1, source_target_pairs={{16,1},{17,2},{18,3},{19,4},{20,5},{21,6},{22,7},{23,8},{24,9},{25... | collective-permute-start | bytes 196616 | tf_op jit(solution)/shard_map/ppermute | solution.py:239
  26.5 23.2 %collective-permute-start = (bf16[8,64,512]{2,1,0:T(8,128)(2,1)}, bf16[8,64,512]{2,1,0:T(8,128)(2,1)S(1)}, u32[]{:S(2)}, u32[]{:S(2)}) collective-permute-start(bf16[8,64,512]{2,1,0:T(8,128)(2,1)} %get-tuple-element.18), channel_id=1, source_target_pairs={{0,16},{1,17},{2,18},{3,19},{4,20},{5,21},{6,22},{7,23},{8,24},{9,... | collective-permute-start | bytes 1572872 | tf_op jit(solution)/shard_map/ppermute | solution.py:239
  30.1 19.5 %collective-permute-start.1 = (bf16[8,64,512]{2,1,0:T(8,128)(2,1)}, bf16[8,64,512]{2,1,0:T(8,128)(2,1)}, u32[]{:S(2)}, u32[]{:S(2)}) collective-permute-start(bf16[8,64,512]{2,1,0:T(8,128)(2,1)} %get-tuple-element.17), channel_id=1, source_target_pairs={{16,0},{17,1},{18,2},{19,3},{20,4},{21,5},{22,6},{23,7},{24,8},{25... | collective-permute-start | bytes 1572872 | tf_op jit(solution)/shard_map/ppermute | solution.py:239
  34.0 15.6 %collective-permute-start.2 = (bf16[16,8,512]{2,1,0:T(8,128)(2,1)}, bf16[16,8,512]{2,1,0:T(8,128)(2,1)S(1)}, u32[]{:S(2)}, u32[]{:S(2)}) collective-permute-start(bf16[16,8,512]{2,1,0:T(8,128)(2,1)} %get-tuple-element.16), channel_id=1, source_target_pairs={{0,1},{1,2},{2,3},{3,4},{4,5},{5,6},{6,7},{7,8},{8,9},{9,10},{10,1... | collective-permute-start | bytes 393224 | tf_op jit(solution)/shard_map/ppermute | solution.py:239
  34.0 15.6 %collective-permute-start.3 = (bf16[16,8,512]{2,1,0:T(8,128)(2,1)}, bf16[16,8,512]{2,1,0:T(8,128)(2,1)S(1)}, u32[]{:S(2)}, u32[]{:S(2)}) collective-permute-start(bf16[16,8,512]{2,1,0:T(8,128)(2,1)} %get-tuple-element.15), channel_id=1, source_target_pairs={{0,15},{1,0},{2,1},{3,2},{4,3},{5,4},{6,5},{7,6},{8,7},{9,8},{10,9... | collective-permute-start | bytes 393224 | tf_op jit(solution)/shard_map/ppermute | solution.py:239
  41.6 8.0 %collective-permute-start.7 = (bf16[8,8,512]{2,1,0:T(8,128)(2,1)}, bf16[8,8,512]{2,1,0:T(8,128)(2,1)S(1)}, u32[]{:S(2)}, u32[]{:S(2)}) collective-permute-start(bf16[8,8,512]{2,1,0:T(8,128)(2,1)} %get-tuple-element.11), channel_id=1, source_target_pairs={{16,15},{17,0},{18,1},{19,2},{20,3},{21,4},{22,5},{23,6},{24,7},{2... | collective-permute-start | bytes 196616 | tf_op jit(solution)/shard_map/ppermute | solution.py:239
  54.4 1.6 %copy-start.5 = (bf16[4,640,512]{2,1,0:T(8,128)(2,1)}, bf16[4,640,512]{2,1,0:T(8,128)(2,1)S(1)}, u32[]{:S(2)}) copy-start(bf16[4,640,512]{2,1,0:T(8,128)(2,1)S(1)} %get-tuple-element.9.k_ref) | copy-start | bytes 7864324
  55.9 1.6 %copy-start.6 = (bf16[4,640,512]{2,1,0:T(8,128)(2,1)}, bf16[4,640,512]{2,1,0:T(8,128)(2,1)S(1)}, u32[]{:S(2)}) copy-start(bf16[4,640,512]{2,1,0:T(8,128)(2,1)S(1)} %get-tuple-element.10.v_ref) | copy-start | bytes 7864324
  57.5 1.0 copy-start.7
Sparse Core Ops, SparseCore 0:
  10.6 73.9 all-gather.1

commit v2 on v0

v2 whole, which is shorter than its diff:
```python
import math

import jax
import jax.numpy as jnp
from jax import lax
from jax.experimental import pallas as pl
from jax.experimental.pallas import tpu as pltpu
from jax.sharding import PartitionSpec as P

BLK = 8
TOK = BLK * BLK
SUMROWS = 4
FAR = 48
EPS = 1e-06
NEG = -1e30
LOG2E = 1.4426950408889634
F32 = jnp.float32
BF16 = jnp.bfloat16
MESH = pl.DeviceIdType.MESH

RING = 4
PARTS = (6, 5, 5)
FIRST = (0, 6, 11)
AXES = (("x", "y", "z"), ("y", "z", "x"), ("z", "x", "y"))
COLS = 8
WIDE = (COLS + 2) * TOK
ROW = COLS * TOK


def rms(wide, gain):
    mean_square = jnp.mean(wide * wide, axis=-1, keepdims=True)
    return (wide * lax.rsqrt(mean_square + EPS) * gain).astype(BF16)


def dot(a, b):
    return jnp.dot(a, b, preferred_element_type=F32)


def summary_row(core, spot, inner):
    row = None
    for part in range(3):
        first, second, third = (spot[axis] for axis in AXES[part])
        place = ((core * RING + third) * RING + second) * RING + first
        here = 128 * FIRST[part] + place * PARTS[part] + inner - FIRST[part]
        row = here if row is None else jnp.where(inner >= FIRST[part], here, row)
    return row


class Gather:
    def __init__(self, ref, send, recv, sib_send, sib_recv, core, spot, lat, lon):
        self.ref = ref
        self.send, self.recv = send, recv
        self.sib_send, self.sib_recv = sib_send, sib_recv
        self.core, self.spot = core, spot
        self.lat, self.lon = lat, lon
        self.started = []

    def device(self, axis, step):
        spot = dict(self.spot)
        spot[axis] = (spot[axis] + step + RING) % RING
        return (2 * spot["z"] + self.core, RING * spot["y"] + spot["x"])

    def rows(self, part, phase, step, half=None, core=None):
        axis = AXES[part][phase]
        spot = dict(self.spot)
        spot[axis] = (spot[axis] + step + RING) % RING
        core = self.core if core is None else core
        place = core
        for level in (2, 1, 0):
            if level >= phase:
                place = place * RING + spot[AXES[part][level]]
        size = PARTS[part] * RING**phase
        start = 128 * FIRST[part] + place * size
        cut = (size + 1) // 2
        if half == 0:
            size = cut
        elif half == 1:
            start, size = start + cut, size - cut
        return pl.ds(start, size)

    def copy(self, rows, send, recv, device):
        return pltpu.make_async_remote_copy(
            src_ref=self.ref.at[rows],
            dst_ref=self.ref.at[rows],
            send_sem=send,
            recv_sem=recv,
            device_id=device,
            device_id_type=MESH,
        )

    def ring(self, part, phase, kind, start):
        axis = AXES[part][phase]
        step = 1 if kind in (0, 2) else -1
        if start:
            origin, half = (0, None) if kind < 2 else (-step, kind - 2)
        else:
            origin, half = (-step, None) if kind < 2 else (-2 * step, kind - 2)
        return self.copy(
            self.rows(part, phase, origin, half),
            self.send.at[part, phase, kind],
            self.recv.at[part, phase, kind],
            self.device(axis, step),
        )

    def sibling(self, part, slot, core):
        if slot == 0:
            rows = self.rows(part, 2, 0, None, core)
        else:
            kind = slot - 1
            step = 1 if kind in (0, 2) else -1
            origin, half = (-step, None) if kind < 2 else (-2 * step, kind - 2)
            rows = self.rows(part, 2, origin, half, core)
        other = (self.lat + 1 - 2 * self.core, self.lon)
        return self.copy(rows, self.sib_send.at[part, slot], self.sib_recv.at[part, slot], other)

    def start_ring(self, phase, kinds):
        for kind in kinds:
            for part in range(3):
                copy = self.ring(part, phase, kind, True)
                copy.start()
                self.started.append(copy)

    def wait_ring(self, phase, kinds):
        for kind in kinds:
            for part in range(3):
                self.ring(part, phase, kind, False).wait_recv()

    def start_sibling(self, slots):
        for slot in slots:
            for part in range(3):
                copy = self.sibling(part, slot, self.core)
                copy.start()
                self.started.append(copy)

    def wait_sibling(self):
        for slot in range(5):
            for part in range(3):
                self.sibling(part, slot, 1 - self.core).wait_recv()

    def finish(self):
        for copy in self.started:
            copy.wait_send()


def layer_kernel(
    idx_ref, scale_ref, bias_ref, gain_ref, mgain_ref, pool_ref,
    tok_hbm, wq_hbm, wk_hbm, wv_hbm, wout_hbm, wup_hbm, wdown_hbm,
    out_ref,
    tok_ref, up_ref, down_ref, left_ref, right_ref, corner_ref,
    wq_ref, wk_ref, wv_ref, wout_ref, wup_ref, wdown_ref,
    every_ref, nb_ref, q_ref, k_ref, v_ref, far_ref, near_ref, high_ref, total_ref, attn_ref,
    load_sem, halo_send, halo_recv, ring_send, ring_recv, sib_send, sib_recv,
):
    lat, lon = lax.axis_index("lat"), lax.axis_index("lon")
    lats, lons = 8, 16
    core = lat % 2
    spot = {"x": lon % RING, "y": lon // RING, "z": lat // 2}
    gather = Gather(every_ref, ring_send, ring_recv, sib_send, sib_recv, core, spot, lat, lon)

    loads = [
        pltpu.make_async_copy(src, dst, load_sem.at[n])
        for n, (src, dst) in enumerate(
            (
                (tok_hbm, tok_ref), (wq_hbm, wq_ref), (wk_hbm, wk_ref), (wv_hbm, wv_ref),
                (wout_hbm, wout_ref), (wup_hbm, wup_ref), (wdown_hbm, wdown_ref),
            )
        )
    ]
    for load in loads:
        load.start()

    def tile(lat_step, lon_step):
        return ((lat + lat_step + lats) % lats, (lon + lon_step + lons) % lons)

    halos = (
        (tok_hbm.at[BLK : 2 * BLK], up_ref, tile(1, 0)),
        (tok_hbm.at[0:BLK], down_ref, tile(-1, 0)),
        (tok_hbm.at[:, COLS - 1], left_ref, tile(0, 1)),
        (tok_hbm.at[:, 0], right_ref, tile(0, -1)),
        (tok_hbm.at[BLK : 2 * BLK, COLS - 1], corner_ref.at[0], tile(1, 1)),
        (tok_hbm.at[BLK : 2 * BLK, 0], corner_ref.at[1], tile(1, -1)),
        (tok_hbm.at[0:BLK, COLS - 1], corner_ref.at[2], tile(-1, 1)),
        (tok_hbm.at[0:BLK, 0], corner_ref.at[3], tile(-1, -1)),
    )
    halo_copies = [
        pltpu.make_async_remote_copy(
            src_ref=src, dst_ref=dst, send_sem=halo_send.at[n], recv_sem=halo_recv.at[n],
            device_id=device, device_id_type=MESH,
        )
        for n, (src, dst, device) in enumerate(halos)
    ]
    partners = [device for _, _, device in halos]
    partners += [gather.device(axis, step) for axis in ("x", "y", "z") for step in (1, -1)]
    partners += [(lat + 1 - 2 * core, lon)]
    barrier = pltpu.get_barrier_semaphore()
    for partner in partners:
        pl.semaphore_signal(barrier, inc=1, device_id=partner, device_id_type=MESH)

    gain = gain_ref[...]
    pool_weight = pool_ref[...]
    loads[0].wait()

    def block_of(ref, first, column):
        return jnp.concatenate([ref[first + r, column].astype(F32) for r in range(BLK)], axis=0)

    for part in range(3):
        base = gather.rows(part, 0, 0).start

        def pool_block(n, carry):
            b = n + FIRST[part]
            i, j = b // COLS, b % COLS
            normed = rms(block_of(tok_ref, i * BLK, j), gain)
            nb_ref[i + 1, pl.ds(pl.multiple_of((j + 1) * TOK, TOK), TOK), :] = normed
            every_ref[base + n] = dot(pool_weight, normed).astype(BF16)
            return carry

        lax.fori_loop(0, PARTS[part], pool_block, 0)
    pl.semaphore_wait(barrier, len(partners))
    for copy in halo_copies:
        copy.start()
    gather.start_ring(0, (0, 1))

    inner = slice(TOK, TOK + ROW)
    loads[1].wait()
    loads[2].wait()
    loads[3].wait()

    def local_qkv(i):
        normed = nb_ref[i + 1, inner, :]
        q_ref[i] = dot(normed, wq_ref[...]).astype(BF16)
        k_ref[i + 1, inner, :] = dot(normed, wk_ref[...]).astype(BF16)
        v_ref[i + 1, inner, :] = dot(normed, wv_ref[...]).astype(BF16)

    local_qkv(0)
    gather.wait_ring(0, (0, 1))
    gather.start_ring(0, (2, 3))
    local_qkv(1)
    gather.wait_ring(0, (2, 3))
    gather.start_ring(1, (0, 1))

    for copy in halo_copies:
        copy.wait_recv()

    def outer_kv(bi, rows):
        normed = nb_ref[bi, rows, :]
        k_ref[bi, rows, :] = dot(normed, wk_ref[...]).astype(BF16)
        v_ref[bi, rows, :] = dot(normed, wv_ref[...]).astype(BF16)

    last = slice(TOK + ROW, WIDE)
    first = slice(0, TOK)

    def outer_row(bi, ref, corner):
        def put(j, carry):
            rows = pl.ds(pl.multiple_of((j + 1) * TOK, TOK), TOK)
            nb_ref[bi, rows, :] = rms(block_of(ref, 0, j), gain)
            return carry

        lax.fori_loop(0, COLS, put, 0, unroll=2)
        for rows, n in ((first, corner), (last, corner + 1)):
            block = jnp.concatenate([corner_ref[n, r].astype(F32) for r in range(BLK)], axis=0)
            nb_ref[bi, rows, :] = rms(block, gain)
        outer_kv(bi, slice(0, WIDE))

    outer_row(0, up_ref, 0)
    gather.wait_ring(1, (0, 1))
    gather.start_ring(1, (2, 3))
    outer_row(3, down_ref, 2)
    for i in range(2):
        for ref, rows in ((left_ref, first), (right_ref, last)):
            block = jnp.concatenate([ref[i * BLK + r].astype(F32) for r in range(BLK)], axis=0)
            nb_ref[i + 1, rows, :] = rms(block, gain)
            outer_kv(i + 1, rows)
    gather.wait_ring(1, (2, 3))
    gather.start_ring(2, (0, 1))
    gather.start_sibling((0,))

    lane_head = lax.broadcasted_iota(jnp.int32, (TOK, 256), 1) // TOK

    def stacked_query(i, rows, feats):
        query = q_ref[i, rows, feats]
        zero = jnp.zeros_like(query)
        return jnp.concatenate([jnp.where(lane_head == h, query, zero) for h in range(4)], axis=0)

    def scores(query, keys):
        return lax.dot_general(query, keys, (((1,), (1,)), ((), ())), preferred_element_type=F32)

    def soft_sum(score, values, scales, bias):
        weights, highs, totals = [], [], []
        for h in range(4):
            part = bias(score[h * TOK : (h + 1) * TOK])
            highest = jnp.max(part, axis=-1, keepdims=True)
            expo = jnp.exp2((part - highest) * scales[h])
            highs.append(highest)
            totals.append(jnp.sum(expo, axis=-1, keepdims=True))
            weights.append(expo.astype(BF16))
        full = dot(jnp.concatenate(weights, axis=0), values)
        picked = full[0:TOK]
        high = jnp.broadcast_to(highs[0], (TOK, 256))
        total = jnp.broadcast_to(totals[0], (TOK, 256))
        for h in range(1, 4):
            mine = lane_head == h
            picked = jnp.where(mine, full[h * TOK : (h + 1) * TOK], picked)
            high = jnp.where(mine, highs[h], high)
            total = jnp.where(mine, totals[h], total)
        return picked, high, total

    def near_block(b, carry):
        i, j = b // COLS, b % COLS
        start = pl.multiple_of(j * TOK, TOK)
        rows = pl.ds(start, TOK)
        around = pl.ds(start, 3 * TOK)
        inside = jnp.where(i == 0, lat > 0, lat < lats - 1)
        edge = jnp.where(inside, jnp.float32(0.0), jnp.float32(NEG))
        for g in range(2):
            feats = slice(g * 256, (g + 1) * 256)
            keys = jnp.concatenate([k_ref[d, around, feats] for d in (1, 2, 3 * i)], axis=0)
            values = jnp.concatenate([v_ref[d, around, feats] for d in (1, 2, 3 * i)], axis=0)
            score = scores(stacked_query(i, rows, feats), keys)
            near_ref[i, rows, feats], high_ref[i, rows, feats], total_ref[i, rows, feats] = soft_sum(
                score, values, [scale_ref[0, g * 4 + h] for h in range(4)],
                lambda part: jnp.concatenate([part[:, :384], part[:, 384:] + edge], axis=1),
            )
        return carry

    lax.fori_loop(0, 8, near_block, 0)
    gather.wait_ring(2, (0, 1))
    gather.start_ring(2, (2, 3))
    gather.start_sibling((1, 2))
    lax.fori_loop(8, 16, near_block, 0)
    gather.wait_ring(2, (2, 3))
    gather.start_sibling((3, 4))
    gather.wait_sibling()

    def far_block(b, carry):
        i, j = b // COLS, b % COLS
        rows = pl.ds(pl.multiple_of(j * TOK, TOK), TOK)
        for s in range(FAR):
            far_ref[s * SUMROWS : (s + 1) * SUMROWS, :] = every_ref[idx_ref[b, s]]
        far = far_ref[...]
        keys = dot(far, wk_ref[...]).astype(BF16)
        values = dot(far, wv_ref[...]).astype(BF16)
        bias = bias_ref[b]
        for g in range(2):
            feats = slice(g * 256, (g + 1) * 256)
            score = scores(stacked_query(i, rows, feats), keys[:, feats])
            scales = [scale_ref[0, g * 4 + h] for h in range(4)]
            far_sum, far_high, far_total = soft_sum(
                score, values[:, feats], scales, lambda part: part + bias
            )
            scale = jnp.full((1, 256), scales[0], F32)
            for h in range(1, 4):
                scale = jnp.where(lane_head[:1] == h, scales[h], scale)
            near_high = high_ref[i, rows, feats]
            high = jnp.maximum(near_high, far_high)
            near_part = jnp.exp2((near_high - high) * scale)
            far_part = jnp.exp2((far_high - high) * scale)
            total = total_ref[i, rows, feats] * near_part + far_total * far_part
            mixed = near_ref[i, rows, feats] * near_part + far_sum * far_part
            attn_ref[i, rows, feats] = (mixed / total).astype(BF16)
        return carry

    lax.fori_loop(0, 16, far_block, 0)

    for load in loads[4:]:
        load.wait()
    mgain = mgain_ref[...]

    def feed_forward(t, carry):
        i, half = t // 2, t % 2
        rows = pl.ds(pl.multiple_of(half * 256, 256), 256)
        token = jnp.concatenate(
            [block_of(tok_ref, i * BLK, half * 4 + j) for j in range(4)], axis=0
        )
        mixed = (token + dot(attn_ref[i, rows, :], wout_ref[...])).astype(BF16)
        wide = mixed.astype(F32)
        normed = rms(wide, mgain)
        acc = wide
        for f in range(4):
            part = slice(f * 512, (f + 1) * 512)
            hidden = jax.nn.gelu(dot(normed, wup_ref[:, part]), approximate=True).astype(BF16)
            acc = acc + dot(hidden, wdown_ref[part, :])
        for r in range(BLK):
            row = jnp.concatenate(
                [acc[j * TOK + r * BLK : j * TOK + (r + 1) * BLK] for j in range(4)], axis=0
            )
            out_ref[i * BLK + r, pl.ds(pl.multiple_of(half * 32, 32), 32), :] = row.astype(BF16)
        return carry

    lax.fori_loop(0, 4, feed_forward, 0)
    for copy in halo_copies:
        copy.wait_send()
    gather.finish()


def layer_call(idx, scale, bias, gain, mgain, pool_weight, tokens, weights):
    rows, cols, feature = tokens.shape
    vmem = pl.BlockSpec(memory_space=pltpu.VMEM)
    smem = pl.BlockSpec(memory_space=pltpu.SMEM)
    hbm = pl.BlockSpec(memory_space=pl.ANY)
    half = (BLK, COLS, BLK, feature)
    dma = pltpu.SemaphoreType.DMA
    return pl.pallas_call(
        layer_kernel,
        out_shape=jax.ShapeDtypeStruct(tokens.shape, BF16),
        in_specs=[smem, smem] + [vmem] * 4 + [hbm] * 7,
        out_specs=vmem,
        scratch_shapes=[
            pltpu.VMEM((2 * BLK, COLS, BLK, feature), BF16),
            pltpu.VMEM(half, BF16),
            pltpu.VMEM(half, BF16),
            pltpu.VMEM((2 * BLK, BLK, feature), BF16),
            pltpu.VMEM((2 * BLK, BLK, feature), BF16),
            pltpu.VMEM((4, BLK, BLK, feature), BF16),
        ]
        + [pltpu.VMEM(weight.shape, BF16) for weight in weights]
        + [
            pltpu.VMEM((2048, SUMROWS, feature), BF16),
            pltpu.VMEM((4, WIDE, feature), BF16),
            pltpu.VMEM((2, ROW, feature), BF16),
            pltpu.VMEM((4, WIDE, feature), BF16),
            pltpu.VMEM((4, WIDE, feature), BF16),
            pltpu.VMEM((FAR * SUMROWS, feature), BF16),
            pltpu.VMEM((2, ROW, feature), F32),
            pltpu.VMEM((2, ROW, feature), F32),
            pltpu.VMEM((2, ROW, feature), F32),
            pltpu.VMEM((2, ROW, feature), BF16),
            dma((7,)), dma((8,)), dma((8,)),
            dma((3, 3, 4)), dma((3, 3, 4)), dma((3, 5)), dma((3, 5)),
        ],
        compiler_params=pltpu.CompilerParams(
            vmem_limit_bytes=60 << 20, collective_id=0, has_side_effects=True
        ),
        name="layer",
    )(
        idx, scale, bias, gain.reshape(1, feature), mgain.reshape(1, feature), pool_weight,
        tokens.reshape(rows, COLS, BLK, feature), *weights,
    )


def local(
    tokens, norm_gain, w_query, w_key, w_value, w_out, pool_weight, head_scale,
    far_ids, far_mask, mlp_gain, w_up, w_down,
):
    rows, cols, feature = tokens.shape
    blk_rows, blk_cols = rows // BLK, cols // BLK
    count = blk_rows * blk_cols
    heads = head_scale.shape[0]
    global_cols = blk_cols * lax.axis_size("lon")
    global_row = far_ids // global_cols
    global_col = far_ids % global_cols
    lat, lon = global_row // blk_rows, global_col // blk_cols
    inner = global_row % blk_rows * blk_cols + global_col % blk_cols
    spot = {"x": lon % RING, "y": lon // RING, "z": lat // 2}
    idx = summary_row(lat % 2, spot, inner).reshape(count, FAR)
    far_valid = jnp.repeat(far_mask.reshape(count, FAR) > 0, SUMROWS, axis=1)
    bias = jnp.where(far_valid, 0.0, NEG).astype(F32)[:, None, :]
    scale = (head_scale * (LOG2E / math.sqrt(feature // heads))).reshape(1, heads)
    return layer_call(
        idx, scale, bias, norm_gain, mlp_gain, pool_weight, tokens,
        (w_query, w_key, w_value, w_out, w_up, w_down),
    )


def solution(mesh):
    return jax.shard_map(
        local,
        mesh=mesh,
        in_specs=(
            P("lat", "lon", None),
            P(), P(), P(), P(), P(), P(), P(),
            P("lat", "lon", None),
            P("lat", "lon", None),
            P(), P(), P(),
        ),
        out_specs=P("lat", "lon", None),
        check_vma=False,
    )
```

time: 539 us -> 82.9 us (0.15); the launches traced: 529 us -> 82.6 us
  local copies, waits for them, and re-layouts: 227 us -> 3.06 us
  other arithmetic: 117 us -> 3.2 us
  matrix products: 92.3 us -> 0 us
  Pallas kernels: 0 us -> 76.3 us
  waiting for transfers between devices: 60.9 us -> 0 us
  between operations: 13.8 us -> 0.02 us
  loops' own time: 9.32 us -> 0 us
  starting transfers between devices: 8.05 us -> 0 us
    dot_general x22 -> x0, matrix products: 92.3 us -> none  [the longest x6 46.7 us: one_row(): jnp.einsum('chqrk,rckhd->cqhd', part_weight, value_grid[:, offset:offset...]
    sub x2 -> x0, other arithmetic: 82.9 us -> none  [one_row(): expo = jnp.exp(jnp.where(keep, score - highest, -1e+30))]
    pallas_call x0 -> x1, Pallas kernels: none -> 76.3 us  [layer_call(): pl.pallas_call(layer_kernel, out_shape=jax.ShapeDtypeStruct(tokens.shape,...]
    reshape x15 -> x0, local copies, waits for them, and re-layouts: 64.7 us -> none  [the longest x6 38.6 us: one_row(): part_score.reshape(blk_cols, head_count, BLK * BLK, near_width)]
    slice x11 -> x0, local copies, waits for them, and re-layouts: 54.7 us -> none  [the longest x8 41.8 us: one_row(): weights[..., offset * near_width:(offset + 1) * near_width]]
    all_gather x1 -> x0, waiting for transfers between devices: 38.2 us -> none  [local(): every_pair = lax.all_gather(summary, ('lat', 'lon'), axis=0, tiled=True)]
    gather x2 -> x0, local copies, waits for them, and re-layouts: 35 us -> none  [local(): far_pair = jnp.take(every_pair, listed_rows, axis=0)]
    dot_general x6 -> x0, local copies, waits for them, and re-layouts: 24 us -> none  [one_row(): jnp.einsum('cqhd,rckhd->chqrk', query_heads, key_grid[:, offset:offset +...]
  transfers between devices with their start and end apart: 5 -> 0, of which waited for: 4 -> 0; matrix products, arithmetic and copies ran while one was open for 3% -> 0% of each run, Pallas kernels for 0% -> 0%
where the time goes in v2:
time: 82.9 us; the launch traced here: 82.6 us
  Pallas kernels  76.3 us (92%)
  other arithmetic  3.2 us (4%)
  local copies, waits for them, and re-layouts  3.06 us (4%)
    pallas_call x1, Pallas kernels, layer_call(): pl.pallas_call(layer_kernel, out_shape=jax.ShapeDtypeStruct(tokens.shape,...  76.3 us
    unnamed x1, local copies, waits for them, and re-layouts  2.29 us

profile of v2, /device:TPU:1, one launch (start us, length us, event | category | flops | bytes accessed | tf_op | source)
XLA Modules:
  0.0 82.6 jit_solution(11251985973065526951)
XLA Ops:
  0.0 1.2 %multiply_bitcast_fusion.scale_ref = f32[1,8]{1,0:T(1,128)} fusion(f32[8]{0:T(128)} %param.20), kind=kLoop, calls=%fused_computation.48 | loop fusion | flops 8 | bytes 64 | tf_op jit(solution)/shard_map/reshape | solution.py:457
  1.2 1.3 %select_bitcast_fusion.1.idx_ref = s32[16,48]{1,0:T(8,128)} fusion(s32[2,8,48]{2,1,0:T(8,128)} %param.21), kind=kLoop, calls=%fused_computation.29 | loop fusion | flops 97536 | bytes 6144 | tf_op jit(solution)/shard_map/reshape | solution.py:454
  2.5 0.7 select_bitcast_fusion
  3.2 0.1 copy.14
  3.3 0.7 copy.15.bias_ref
  4.0 76.3 %layer.1 = bf16[16,64,512]{2,1,0:T(8,128)(2,1)} custom-call(s32[16,48]{1,0:T(8,128)} %select_bitcast_fusion.1.idx_ref, f32[1,8]{1,0:T(1,128)} %multiply_bitcast_fusion.scale_ref, f32[16,1,192]{2,1,0:T(1,128)} %copy.15.bias_ref, f32[1,512]{1,0:T(1,128)} %bitcast.12, f32[1,512]{1,0:T(1,128)} %bitcast.13, bf16[4,64]{1,0:T(4,128)(2,1)} %pool_ref.1, ...), custom_call_target="tpu_custom_call" | custom-call | tf_op jit(solution)/shard_map/layer/pallas_call | solution.py:402
  80.3 2.3 %copy.17 = bf16[16,64,512]{2,1,0:T(8,128)(2,1)} copy(bf16[16,64,512]{2,1,0:T(8,128)(2,1)} %layer.1) | data formatting | bytes 2097152
  (1 shorter events, 0.0 us)

commit v3 on v2

--- a/solution.py
+++ b/solution.py
@@ -13,14 +13,15 @@
 FAR = 48
 EPS = 1e-06
 NEG = -1e30
-LOG2E = 1.4426950408889634
+SCALE = 1.4426950408889634 / math.sqrt(64)
+PUMP_A, PUMP_B, PUMP_C, PUMP_D = 1, 4, 7, 10
 F32 = jnp.float32
 BF16 = jnp.bfloat16
 MESH = pl.DeviceIdType.MESH
 
 RING = 4
-PARTS = (6, 5, 5)
-FIRST = (0, 6, 11)
+PARTS = (4, 5, 7)
+FIRST = (0, 4, 9)
 AXES = (("x", "y", "z"), ("y", "z", "x"), ("z", "x", "y"))
 COLS = 8
 WIDE = (COLS + 2) * TOK
@@ -47,115 +48,154 @@
 
 
 class Gather:
-    def __init__(self, ref, send, recv, sib_send, sib_recv, core, spot, lat, lon):
+    SUBS = (0, -1, 1, 2)
+    HOPS = (1, -1, 2)
+
+    def __init__(self, ref, sems, core, spot, lat, lon):
         self.ref = ref
-        self.send, self.recv = send, recv
-        self.sib_send, self.sib_recv = sib_send, sib_recv
+        self.sems = sems
         self.core, self.spot = core, spot
-        self.lat, self.lon = lat, lon
-        self.started = []
+        self.other = (lat + 1 - 2 * core, lon)
+        self.makers = []
 
     def device(self, axis, step):
         spot = dict(self.spot)
         spot[axis] = (spot[axis] + step + RING) % RING
         return (2 * spot["z"] + self.core, RING * spot["y"] + spot["x"])
 
-    def rows(self, part, phase, step, half=None, core=None):
-        axis = AXES[part][phase]
-        spot = dict(self.spot)
-        spot[axis] = (spot[axis] + step + RING) % RING
-        core = self.core if core is None else core
-        place = core
-        for level in (2, 1, 0):
-            if level >= phase:
-                place = place * RING + spot[AXES[part][level]]
-        size = PARTS[part] * RING**phase
+    def rows(self, part, level, steps, half=None, core=None):
+        place = self.core if core is None else core
+        for at in (2, 1, 0):
+            if at >= level:
+                place = place * RING + (self.spot[AXES[part][at]] + steps.get(at, 0) + RING) % RING
+        size = PARTS[part] * RING**level
         start = 128 * FIRST[part] + place * size
-        cut = (size + 1) // 2
-        if half == 0:
-            size = cut
-        elif half == 1:
-            start, size = start + cut, size - cut
+        if half is not None:
+            cut = (size + 1) // 2
+            start, size = (start, cut) if half == 0 else (start + cut, size - cut)
         return pl.ds(start, size)
 
-    def copy(self, rows, send, recv, device):
+    def copy(self, name, index, rows, device):
+        send, recv = self.sems[name]
         return pltpu.make_async_remote_copy(
             src_ref=self.ref.at[rows],
             dst_ref=self.ref.at[rows],
-            send_sem=send,
-            recv_sem=recv,
+            send_sem=send.at[index],
+            recv_sem=recv.at[index],
             device_id=device,
             device_id_type=MESH,
         )
 
-    def ring(self, part, phase, kind, start):
-        axis = AXES[part][phase]
-        step = 1 if kind in (0, 2) else -1
-        if start:
-            origin, half = (0, None) if kind < 2 else (-step, kind - 2)
-        else:
-            origin, half = (-step, None) if kind < 2 else (-2 * step, kind - 2)
-        return self.copy(
-            self.rows(part, phase, origin, half),
-            self.send.at[part, phase, kind],
-            self.recv.at[part, phase, kind],
-            self.device(axis, step),
-        )
-
-    def sibling(self, part, slot, core):
-        if slot == 0:
-            rows = self.rows(part, 2, 0, None, core)
-        else:
-            kind = slot - 1
-            step = 1 if kind in (0, 2) else -1
-            origin, half = (-step, None) if kind < 2 else (-2 * step, kind - 2)
-            rows = self.rows(part, 2, origin, half, core)
-        other = (self.lat + 1 - 2 * self.core, self.lon)
-        return self.copy(rows, self.sib_send.at[part, slot], self.sib_recv.at[part, slot], other)
-
-    def start_ring(self, phase, kinds):
-        for kind in kinds:
-            for part in range(3):
-                copy = self.ring(part, phase, kind, True)
-                copy.start()
-                self.started.append(copy)
-
-    def wait_ring(self, phase, kinds):
-        for kind in kinds:
-            for part in range(3):
-                self.ring(part, phase, kind, False).wait_recv()
+    def go(self, name, index, where, target):
+        self.makers.append((name, index, where, target))
+        self.make(name, index, where, target).start()
+
+    def make(self, name, index, where, target):
+        device = self.other if target is None else self.device(*target)
+        return self.copy(name, index, self.rows(*where), device)
+
+    def finish(self):
+        for spec in self.makers:
+            self.make(*spec).wait_send()
+
+    def take(self, name, index, where):
+        self.copy(name, index, self.rows(*where), self.other).wait_recv()
+
+    def start_first(self):
+        for n, hop in enumerate(self.HOPS):
+            for part in range(3):
+                self.go("first", (part, n), (part, 0, {}), (AXES[part][0], hop))
+
+    def wait_first(self):
+        for n, hop in enumerate(self.HOPS):
+            for part in range(3):
+                self.take("first", (part, n), (part, 0, {0: -hop}))
+
+    def start_second(self):
+        for kind, step in enumerate((1, -1)):
+            for part in range(3):
+                self.go("second", (part, kind), (part, 1, {}), (AXES[part][1], step))
+
+    def wait_second(self):
+        for kind, step in enumerate((1, -1)):
+            for part in range(3):
+                self.take("second", (part, kind), (part, 1, {1: -step}))
+
+    def start_second_on(self):
+        for kind, step in enumerate((1, -1)):
+            for part in range(3):
+                self.go(
+                    "second", (part, kind + 2), (part, 1, {1: -step}, kind), (AXES[part][1], step)
+                )
+
+    def wait_second_on(self):
+        for kind, step in enumerate((1, -1)):
+            for part in range(3):
+                self.take("second", (part, kind + 2), (part, 1, {1: -2 * step}, kind))
+
+    def start_third(self, subs):
+        for n in subs:
+            for kind, step in enumerate((1, -1)):
+                for part in range(3):
+                    self.go(
+                        "third", (part, n, kind), (part, 1, {1: self.SUBS[n]}), (AXES[part][2], step)
+                    )
+
+    def wait_third(self, subs):
+        for n in subs:
+            for kind, step in enumerate((1, -1)):
+                for part in range(3):
+                    self.take(
+                        "third", (part, n, kind), (part, 1, {1: self.SUBS[n], 2: -step})
+                    )
+
+    def start_third_on(self, subs):
+        for n in subs:
+            step = 1 if n in (0, 2) else -1
+            for part in range(3):
+                self.go(
+                    "on", (part, n), (part, 1, {1: self.SUBS[n], 2: -step}), (AXES[part][2], step)
+                )
+
+    def wait_third_on(self, subs):
+        for n in subs:
+            step = 1 if n in (0, 2) else -1
+            for part in range(3):
+                self.take("on", (part, n), (part, 1, {1: self.SUBS[n], 2: -2 * step}))
+
+    def sibling_where(self, part, slot, core):
+        if slot < 3:
+            return (part, 2, {2: (0, -1, 1)[slot]}, None, core)
+        return (part, 1, {1: self.SUBS[slot - 3], 2: 2}, None, core)
 
     def start_sibling(self, slots):
         for slot in slots:
             for part in range(3):
-                copy = self.sibling(part, slot, self.core)
-                copy.start()
-                self.started.append(copy)
-
-    def wait_sibling(self):
-        for slot in range(5):
-            for part in range(3):
-                self.sibling(part, slot, 1 - self.core).wait_recv()
-
-    def finish(self):
-        for copy in self.started:
-            copy.wait_send()
+                self.go("core", (part, slot), self.sibling_where(part, slot, self.core), None)
+
+    def wait_sibling(self, slots):
+        for slot in slots:
+            for part in range(3):
+                self.take("core", (part, slot), self.sibling_where(part, slot, 1 - self.core))
 
 
 def layer_kernel(
-    idx_ref, scale_ref, bias_ref, gain_ref, mgain_ref, pool_ref,
+    head_ref, ids_ref, mask_ref, gain_ref, mgain_ref, pool_ref,
     tok_hbm, wq_hbm, wk_hbm, wv_hbm, wout_hbm, wup_hbm, wdown_hbm,
     out_ref,
     tok_ref, up_ref, down_ref, left_ref, right_ref, corner_ref,
     wq_ref, wk_ref, wv_ref, wout_ref, wup_ref, wdown_ref,
     every_ref, nb_ref, q_ref, k_ref, v_ref, far_ref, near_ref, high_ref, total_ref, attn_ref,
-    load_sem, halo_send, halo_recv, ring_send, ring_recv, sib_send, sib_recv,
+    rows_ref, idx_ref, bias_ref,
+    load_sem, halo_send, halo_recv, *ring_sems,
 ):
     lat, lon = lax.axis_index("lat"), lax.axis_index("lon")
     lats, lons = 8, 16
     core = lat % 2
     spot = {"x": lon % RING, "y": lon // RING, "z": lat // 2}
-    gather = Gather(every_ref, ring_send, ring_recv, sib_send, sib_recv, core, spot, lat, lon)
+    names = ("first", "second", "third", "on", "core")
+    sems = {name: (ring_sems[2 * n], ring_sems[2 * n + 1]) for n, name in enumerate(names)}
+    gather = Gather(every_ref, sems, core, spot, lat, lon)
 
     loads = [
         pltpu.make_async_copy(src, dst, load_sem.at[n])
@@ -190,7 +230,7 @@
         for n, (src, dst, device) in enumerate(halos)
     ]
     partners = [device for _, _, device in halos]
-    partners += [gather.device(axis, step) for axis in ("x", "y", "z") for step in (1, -1)]
+    partners += [gather.device(axis, step) for axis in ("x", "y", "z") for step in (1, -1, 2)]
     partners += [(lat + 1 - 2 * core, lon)]
     barrier = pltpu.get_barrier_semaphore()
     for partner in partners:
@@ -198,13 +238,31 @@
 
     gain = gain_ref[...]
     pool_weight = pool_ref[...]
+
+    ids = ids_ref[...]
+    grow, gcol = ids >> 7, ids & 127
+    to_lat, to_lon = grow >> 1, gcol >> 3
+    to_spot = {"x": to_lon & 3, "y": to_lon >> 2, "z": to_lat >> 1}
+    rows_ref[...] = jnp.zeros_like(rows_ref)
+    rows_ref[:, :FAR] = summary_row(to_lat & 1, to_spot, (grow & 1) * COLS + (gcol & 7))
+    index_load = pltpu.make_async_copy(rows_ref, idx_ref, load_sem.at[7])
+    index_load.start()
+    slot = lax.broadcasted_iota(jnp.int32, (FAR, FAR * SUMROWS), 0)
+    key = lax.broadcasted_iota(jnp.int32, (FAR, FAR * SUMROWS), 1)
+    spread = jnp.where(key // SUMROWS == slot, 1.0, 0.0).astype(BF16)
+    used = jnp.where(mask_ref[...] > 0, 1.0, 0.0).astype(BF16)
+    bias_ref[...] = jnp.where(dot(used, spread) > 0.5, 0.0, NEG)
+
+    pl.semaphore_wait(barrier, len(partners))
+    for copy in halo_copies:
+        copy.start()
     loads[0].wait()
 
     def block_of(ref, first, column):
         return jnp.concatenate([ref[first + r, column].astype(F32) for r in range(BLK)], axis=0)
 
     for part in range(3):
-        base = gather.rows(part, 0, 0).start
+        base = gather.rows(part, 0, {}).start
 
         def pool_block(n, carry):
             b = n + FIRST[part]
@@ -215,10 +273,7 @@
             return carry
 
         lax.fori_loop(0, PARTS[part], pool_block, 0)
-    pl.semaphore_wait(barrier, len(partners))
-    for copy in halo_copies:
-        copy.start()
-    gather.start_ring(0, (0, 1))
+    gather.start_first()
 
     inner = slice(TOK, TOK + ROW)
     loads[1].wait()
@@ -232,11 +287,13 @@
         v_ref[i + 1, inner, :] = dot(normed, wv_ref[...]).astype(BF16)
 
     local_qkv(0)
-    gather.wait_ring(0, (0, 1))
-    gather.start_ring(0, (2, 3))
+    gather.wait_first()
+    gather.start_second()
+    gather.start_third((0,))
     local_qkv(1)
-    gather.wait_ring(0, (2, 3))
-    gather.start_ring(1, (0, 1))
+    gather.wait_second()
+    gather.start_second_on()
+    gather.start_third((1, 2))
 
     for copy in halo_copies:
         copy.wait_recv()
@@ -262,17 +319,17 @@
         outer_kv(bi, slice(0, WIDE))
 
     outer_row(0, up_ref, 0)
-    gather.wait_ring(1, (0, 1))
-    gather.start_ring(1, (2, 3))
+    gather.wait_second_on()
+    gather.start_third((3,))
+    gather.start_sibling((0,))
+    gather.wait_third((0,))
+    gather.start_third_on((0,))
     outer_row(3, down_ref, 2)
     for i in range(2):
         for ref, rows in ((left_ref, first), (right_ref, last)):
             block = jnp.concatenate([ref[i * BLK + r].astype(F32) for r in range(BLK)], axis=0)
             nb_ref[i + 1, rows, :] = rms(block, gain)
             outer_kv(i + 1, rows)
-    gather.wait_ring(1, (2, 3))
-    gather.start_ring(2, (0, 1))
-    gather.start_sibling((0,))
 
     lane_head = lax.broadcasted_iota(jnp.int32, (TOK, 256), 1) // TOK
 
@@ -317,19 +374,38 @@
             values = jnp.concatenate([v_ref[d, around, feats] for d in (1, 2, 3 * i)], axis=0)
             score = scores(stacked_query(i, rows, feats), keys)
             near_ref[i, rows, feats], high_ref[i, rows, feats], total_ref[i, rows, feats] = soft_sum(
-                score, values, [scale_ref[0, g * 4 + h] for h in range(4)],
+                score, values, [head_ref[0, g * 4 + h] * SCALE for h in range(4)],
                 lambda part: jnp.concatenate([part[:, :384], part[:, 384:] + edge], axis=1),
             )
         return carry
 
-    lax.fori_loop(0, 8, near_block, 0)
-    gather.wait_ring(2, (0, 1))
-    gather.start_ring(2, (2, 3))
-    gather.start_sibling((1, 2))
-    lax.fori_loop(8, 16, near_block, 0)
-    gather.wait_ring(2, (2, 3))
-    gather.start_sibling((3, 4))
-    gather.wait_sibling()
+    def pump_a():
+        gather.wait_third((1, 2))
+        gather.start_third_on((1, 2))
+
+    def pump_b():
+        gather.wait_third((3,))
+        gather.start_third_on((3,))
+        gather.start_sibling((1, 2))
+
+    def pump_c():
+        gather.wait_third_on((0, 1))
+        gather.start_sibling((3, 4))
+
+    def pump_d():
+        gather.wait_third_on((2, 3))
+        gather.start_sibling((5, 6))
+
+    pumps = ((PUMP_A, pump_a), (PUMP_B, pump_b), (PUMP_C, pump_c), (PUMP_D, pump_d))
+
+    def near_step(b, carry):
+        for when, pump in pumps:
+            pl.when(b == when)(pump)
+        return near_block(b, carry)
+
+    lax.fori_loop(0, 16, near_step, 0)
+    gather.wait_sibling(range(7))
+    index_load.wait()
 
     def far_block(b, carry):
         i, j = b // COLS, b % COLS
@@ -339,11 +415,11 @@
         far = far_ref[...]
         keys = dot(far, wk_ref[...]).astype(BF16)
         values = dot(far, wv_ref[...]).astype(BF16)
-        bias = bias_ref[b]
+        bias = bias_ref[pl.ds(b, 1), :]
         for g in range(2):
             feats = slice(g * 256, (g + 1) * 256)
             score = scores(stacked_query(i, rows, feats), keys[:, feats])
-            scales = [scale_ref[0, g * 4 + h] for h in range(4)]
+            scales = [head_ref[0, g * 4 + h] * SCALE for h in range(4)]
             far_sum, far_high, far_total = soft_sum(
                 score, values[:, feats], scales, lambda part: part + bias
             )
@@ -392,7 +468,7 @@
     gather.finish()
 
 
-def layer_call(idx, scale, bias, gain, mgain, pool_weight, tokens, weights):
+def layer_call(head_scale, ids, mask, gain, mgain, pool_weight, tokens, weights):
     rows, cols, feature = tokens.shape
     vmem = pl.BlockSpec(memory_space=pltpu.VMEM)
     smem = pl.BlockSpec(memory_space=pltpu.SMEM)
@@ -402,7 +478,7 @@
     return pl.pallas_call(
         layer_kernel,
         out_shape=jax.ShapeDtypeStruct(tokens.shape, BF16),
-        in_specs=[smem, smem] + [vmem] * 4 + [hbm] * 7,
+        in_specs=[smem] + [vmem] * 5 + [hbm] * 7,
         out_specs=vmem,
         scratch_shapes=[
             pltpu.VMEM((2 * BLK, COLS, BLK, feature), BF16),
@@ -424,15 +500,18 @@
             pltpu.VMEM((2, ROW, feature), F32),
             pltpu.VMEM((2, ROW, feature), F32),
             pltpu.VMEM((2, ROW, feature), BF16),
-            dma((7,)), dma((8,)), dma((8,)),
-            dma((3, 3, 4)), dma((3, 3, 4)), dma((3, 5)), dma((3, 5)),
-        ],
+            pltpu.VMEM((2 * COLS, 128), jnp.int32),
+            pltpu.SMEM((2 * COLS, 128), jnp.int32),
+            pltpu.VMEM((2 * COLS, FAR * SUMROWS), F32),
+            dma((8,)), dma((8,)), dma((8,)),
+        ]
+        + [dma(shape) for shape in ((3, 3), (3, 4), (3, 4, 2), (3, 4), (3, 7)) for _ in range(2)],
         compiler_params=pltpu.CompilerParams(
             vmem_limit_bytes=60 << 20, collective_id=0, has_side_effects=True
         ),
         name="layer",
     )(
-        idx, scale, bias, gain.reshape(1, feature), mgain.reshape(1, feature), pool_weight,
+        head_scale, ids, mask, gain.reshape(1, feature), mgain.reshape(1, feature), pool_weight,
         tokens.reshape(rows, COLS, BLK, feature), *weights,
     )
 
@@ -441,22 +520,9 @@
     tokens, norm_gain, w_query, w_key, w_value, w_out, pool_weight, head_scale,
     far_ids, far_mask, mlp_gain, w_up, w_down,
 ):
-    rows, cols, feature = tokens.shape
-    blk_rows, blk_cols = rows // BLK, cols // BLK
-    count = blk_rows * blk_cols
-    heads = head_scale.shape[0]
-    global_cols = blk_cols * lax.axis_size("lon")
-    global_row = far_ids // global_cols
-    global_col = far_ids % global_cols
-    lat, lon = global_row // blk_rows, global_col // blk_cols
-    inner = global_row % blk_rows * blk_cols + global_col % blk_cols
-    spot = {"x": lon % RING, "y": lon // RING, "z": lat // 2}
-    idx = summary_row(lat % 2, spot, inner).reshape(count, FAR)
-    far_valid = jnp.repeat(far_mask.reshape(count, FAR) > 0, SUMROWS, axis=1)
-    bias = jnp.where(far_valid, 0.0, NEG).astype(F32)[:, None, :]
-    scale = (head_scale * (LOG2E / math.sqrt(feature // heads))).reshape(1, heads)
     return layer_call(
-        idx, scale, bias, norm_gain, mlp_gain, pool_weight, tokens,
+        head_scale.reshape(1, -1), far_ids.reshape(-1, FAR), far_mask.reshape(-1, FAR),
+        norm_gain, mlp_gain, pool_weight, tokens,
         (w_query, w_key, w_value, w_out, w_up, w_down),
     )
 

time: 82.9 us -> 77 us (0.929)
  other arithmetic: 3.2 us -> 0 us
  Pallas kernels: 76.3 us -> 74.5 us
    reshape x2 -> x0, other arithmetic: 2.51 us -> none  [the longest x1 1.34 us: local(): idx = summary_row(lat % 2, spot, inner).reshape(count, FAR)]
    pallas_call x1, Pallas kernels: 76.3 us -> 74.5 us  [layer_call(): pl.pallas_call(layer_kernel, out_shape=jax.ShapeDtypeStruct(tokens.shape,...]
where the time goes in v3:
time: 77 us; the launch traced here: 76.8 us
  Pallas kernels  74.5 us (97%)
  local copies, waits for them, and re-layouts  2.29 us (3%)
    pallas_call x1, Pallas kernels, layer_call(): pl.pallas_call(layer_kernel, out_shape=jax.ShapeDtypeStruct(tokens.shape,...  74.5 us
    unnamed x1, local copies, waits for them, and re-layouts  2.29 us

profile of v3, /device:TPU:1, one launch (start us, length us, event | category | flops | bytes accessed | tf_op | source)
XLA Modules:
  0.0 76.8 jit_solution(11147501390970398751)
XLA Ops:
  0.0 74.5 %layer.1 = bf16[16,64,512]{2,1,0:T(8,128)(2,1)} custom-call(f32[1,8]{1,0:T(1,128)} %bitcast.11, s32[16,48]{1,0:T(8,128)} %bitcast.7, s32[16,48]{1,0:T(8,128)} %bitcast.8, f32[1,512]{1,0:T(1,128)} %bitcast.9, f32[1,512]{1,0:T(1,128)} %bitcast.10, bf16[4,64]{1,0:T(4,128)(2,1)} %pool_ref.1, bf16[16,8,8,512]{3,2,1,0:T(8,128)(2,1)} %bitcast.6, ...), custom_call_target="tpu_custom_call" | custom-call | tf_op jit(solution)/shard_map/layer/pallas_call | solution.py:478
  74.5 2.3 %copy.15 = bf16[16,64,512]{2,1,0:T(8,128)(2,1)} copy(bf16[16,64,512]{2,1,0:T(8,128)(2,1)} %layer.1) | data formatting | bytes 2097152

commit v4 on v3

--- a/solution.py
+++ b/solution.py
@@ -14,7 +14,7 @@
 EPS = 1e-06
 NEG = -1e30
 SCALE = 1.4426950408889634 / math.sqrt(64)
-PUMP_A, PUMP_B, PUMP_C, PUMP_D = 1, 4, 7, 10
+PUMP_S, PUMP_A, PUMP_B, PUMP_C, PUMP_D = 1, 4, 7, 10, 13
 F32 = jnp.float32
 BF16 = jnp.bfloat16
 MESH = pl.DeviceIdType.MESH
@@ -253,9 +253,6 @@
     used = jnp.where(mask_ref[...] > 0, 1.0, 0.0).astype(BF16)
     bias_ref[...] = jnp.where(dot(used, spread) > 0.5, 0.0, NEG)
 
-    pl.semaphore_wait(barrier, len(partners))
-    for copy in halo_copies:
-        copy.start()
     loads[0].wait()
 
     def block_of(ref, first, column):
@@ -273,7 +270,10 @@
             return carry
 
         lax.fori_loop(0, PARTS[part], pool_block, 0)
+    pl.semaphore_wait(barrier, len(partners))
     gather.start_first()
+    for copy in halo_copies:
+        copy.start()
 
     inner = slice(TOK, TOK + ROW)
     loads[1].wait()
@@ -291,9 +291,6 @@
     gather.start_second()
     gather.start_third((0,))
     local_qkv(1)
-    gather.wait_second()
-    gather.start_second_on()
-    gather.start_third((1, 2))
 
     for copy in halo_copies:
         copy.wait_recv()
@@ -319,11 +316,9 @@
         outer_kv(bi, slice(0, WIDE))
 
     outer_row(0, up_ref, 0)
-    gather.wait_second_on()
-    gather.start_third((3,))
-    gather.start_sibling((0,))
-    gather.wait_third((0,))
-    gather.start_third_on((0,))
+    gather.wait_second()
+    gather.start_second_on()
+    gather.start_third((1, 2))
     outer_row(3, down_ref, 2)
     for i in range(2):
         for ref, rows in ((left_ref, first), (right_ref, last)):
@@ -379,6 +374,13 @@
             )
         return carry
 
+    def pump_s():
+        gather.wait_second_on()
+        gather.start_third((3,))
+        gather.start_sibling((0,))
+        gather.wait_third((0,))
+        gather.start_third_on((0,))
+
     def pump_a():
         gather.wait_third((1, 2))
         gather.start_third_on((1, 2))
@@ -396,7 +398,7 @@
         gather.wait_third_on((2, 3))
         gather.start_sibling((5, 6))
 
-    pumps = ((PUMP_A, pump_a), (PUMP_B, pump_b), (PUMP_C, pump_c), (PUMP_D, pump_d))
+    pumps = ((PUMP_S, pump_s), (PUMP_A, pump_a), (PUMP_B, pump_b), (PUMP_C, pump_c), (PUMP_D, pump_d))
 
     def near_step(b, carry):
         for when, pump in pumps:

time: 77 us -> 71.9 us (0.934)
  Pallas kernels: 74.5 us -> 68.9 us
    pallas_call x1, Pallas kernels: 74.5 us -> 68.9 us  [layer_call(): pl.pallas_call(layer_kernel, out_shape=jax.ShapeDtypeStruct(tokens.shape,...]
where the time goes in v4:
time: 71.9 us; the launch traced here: 71.2 us
  Pallas kernels  68.9 us (96%)
  local copies, waits for them, and re-layouts  2.29 us (3%)
    pallas_call x1, Pallas kernels, layer_call(): pl.pallas_call(layer_kernel, out_shape=jax.ShapeDtypeStruct(tokens.shape,...  68.9 us
    unnamed x1, local copies, waits for them, and re-layouts  2.29 us

profile of v4, /device:TPU:1, one launch (start us, length us, event | category | flops | bytes accessed | tf_op | source)
XLA Modules:
  0.0 71.2 jit_solution(2120489630851623068)
XLA Ops:
  0.0 68.9 %layer.1 = bf16[16,64,512]{2,1,0:T(8,128)(2,1)} custom-call(f32[1,8]{1,0:T(1,128)} %bitcast.11, s32[16,48]{1,0:T(8,128)} %bitcast.7, s32[16,48]{1,0:T(8,128)} %bitcast.8, f32[1,512]{1,0:T(1,128)} %bitcast.9, f32[1,512]{1,0:T(1,128)} %bitcast.10, bf16[4,64]{1,0:T(4,128)(2,1)} %pool_ref.1, bf16[16,8,8,512]{3,2,1,0:T(8,128)(2,1)} %bitcast.6, ...), custom_call_target="tpu_custom_call" | custom-call | tf_op jit(solution)/shard_map/layer/pallas_call | solution.py:480
  68.9 2.3 %copy.15 = bf16[16,64,512]{2,1,0:T(8,128)(2,1)} copy(bf16[16,64,512]{2,1,0:T(8,128)(2,1)} %layer.1) | data formatting | bytes 2097152

commit v5 on v4

--- a/solution.py
+++ b/solution.py
@@ -14,7 +14,7 @@
 EPS = 1e-06
 NEG = -1e30
 SCALE = 1.4426950408889634 / math.sqrt(64)
-PUMP_S, PUMP_A, PUMP_B, PUMP_C, PUMP_D = 1, 4, 7, 10, 13
+PUMP_S, PUMP_A, PUMP_B, PUMP_C, PUMP_D = 2, 6, 9, 12, 14
 F32 = jnp.float32
 BF16 = jnp.bfloat16
 MESH = pl.DeviceIdType.MESH
@@ -269,7 +269,7 @@
             every_ref[base + n] = dot(pool_weight, normed).astype(BF16)
             return carry
 
-        lax.fori_loop(0, PARTS[part], pool_block, 0)
+        lax.fori_loop(0, PARTS[part], pool_block, 0, unroll=True)
     pl.semaphore_wait(barrier, len(partners))
     gather.start_first()
     for copy in halo_copies:
@@ -437,7 +437,7 @@
             attn_ref[i, rows, feats] = (mixed / total).astype(BF16)
         return carry
 
-    lax.fori_loop(0, 16, far_block, 0)
+    lax.fori_loop(0, 16, far_block, 0, unroll=2)
 
     for load in loads[4:]:
         load.wait()
@@ -464,7 +464,7 @@
             out_ref[i * BLK + r, pl.ds(pl.multiple_of(half * 32, 32), 32), :] = row.astype(BF16)
         return carry
 
-    lax.fori_loop(0, 4, feed_forward, 0)
+    lax.fori_loop(0, 4, feed_forward, 0, unroll=2)
     for copy in halo_copies:
         copy.wait_send()
     gather.finish()

time: 71.9 us -> 68.3 us (0.950)
  Pallas kernels: 68.9 us -> 65.8 us
    pallas_call x1, Pallas kernels: 68.9 us -> 65.8 us  [layer_call(): pl.pallas_call(layer_kernel, out_shape=jax.ShapeDtypeStruct(tokens.shape,...]
where the time goes in v5:
time: 68.3 us; the launch traced here: 68.1 us
  Pallas kernels  65.8 us (96%)
  local copies, waits for them, and re-layouts  2.29 us (3%)
    pallas_call x1, Pallas kernels, layer_call(): pl.pallas_call(layer_kernel, out_shape=jax.ShapeDtypeStruct(tokens.shape,...  65.8 us
    unnamed x1, local copies, waits for them, and re-layouts  2.29 us

profile of v5, /device:TPU:1, one launch (start us, length us, event | category | flops | bytes accessed | tf_op | source)
XLA Modules:
  0.0 68.1 jit_solution(18271846193668789186)
XLA Ops:
  0.0 65.8 %layer.1 = bf16[16,64,512]{2,1,0:T(8,128)(2,1)} custom-call(f32[1,8]{1,0:T(1,128)} %bitcast.11, s32[16,48]{1,0:T(8,128)} %bitcast.7, s32[16,48]{1,0:T(8,128)} %bitcast.8, f32[1,512]{1,0:T(1,128)} %bitcast.9, f32[1,512]{1,0:T(1,128)} %bitcast.10, bf16[4,64]{1,0:T(4,128)(2,1)} %pool_ref.1, bf16[16,8,8,512]{3,2,1,0:T(8,128)(2,1)} %bitcast.6, ...), custom_call_target="tpu_custom_call" | custom-call | tf_op jit(solution)/shard_map/layer/pallas_call | solution.py:480
  65.8 2.3 %copy.15 = bf16[16,64,512]{2,1,0:T(8,128)(2,1)} copy(bf16[16,64,512]{2,1,0:T(8,128)(2,1)} %layer.1) | data formatting | bytes 2097152
